TPU v7x, 128 devices: a whole 4x4x4 slice. The times are simulated.
128 devices in a mesh: wide: 16 (over z, x), narrow: 8 (over y, core).
Axes of the slice: x: 4, y: 4, z: 4, core: 2. Of those that a mesh axis runs over, the one named last changes fastest.
Arguments:
- depth_start: float32 [2048, 4096], P('wide', 'narrow'), may hold values from 0.1 to 1
- conveyance: float32 [2048, 4096], P('wide', 'narrow'), may hold values from 0.5 to 4
- cell_rain: float32 [2048, 4096], P('wide', 'narrow'), may hold values from 0.01 to 0.2
- nitrogen: float32 [2048, 4096], P('wide', 'narrow'), may hold values from 0.1 to 2
- flow_dir: int32 [2048, 4096], P('wide', 'narrow'), may hold values from 0 to 3
- unit_hydro: float32 [512], replicated, as said below
- rain_hours: bfloat16 [8, 32768, 512], P('narrow', 'wide'), may hold values from 0.049804688 to 2
- send_rows: int32 [8, 5, 16, 128], P('narrow', None, 'wide'), may hold values from -1 to 2047, as said below
- send_owner: int32 [8, 5, 16, 128], P('narrow', None, 'wide'), may hold values from -1 to 15, as said below
- send_down: int32 [8, 5, 16, 128], P('narrow', None, 'wide'), may hold values from -1 to 2047, as said below
Outputs:
- water_depth: float32 [2048, 4096], P('wide', 'narrow')
- nitrogen_left: float32 [2048, 4096], P('wide', 'narrow')
- discharge: float32 [8, 32768, 512], P('narrow', 'wide')
Inputs may be any that keep to these rules, and one draw needn't show every extreme that they name: `unit_hydro`: positive weights of the unit hydrograph. send_rows[g, l, w, :] lists distinct local rows of owner w that send at level l, used slots first and -1 after; every owner sends at least 64 rows at each level, and some owner exactly 128; no row sends at two levels, and a row that receives at level l sends at no level up to l. `send_owner`: -1 exactly where send_rows is -1; at each level at most 16 rows of one owner go to the same owner, and one owner receives exactly 16 rows from every owner. `send_down`: -1 exactly where send_rows is -1.
All inputs are finite; a program needn't handle non-finite values.
Results may differ from a plain program's by a relative error of at most 0.00051.
Values sent between devices are 32-bit elements; how exact they have to be, the bound alone decides.
No kernel may reach another device: no remote copies, remote signals or barrier semaphores. Data moves between devices by JAX's collectives and lax.ppermute only.
A program may use at most 64 MiB of HBM per device.

v0:
```python
import jax
import jax.numpy as jnp
from jax import lax
from jax.sharding import PartitionSpec as P

SUB_ROWS = 2
SUB_COLS = 16
STEPS = 4


WASH = 1.5
RECENT = 0.6
EARLIER = 0.3
EXACT = lax.Precision.HIGHEST


def extended_2(array, sides, width):
    for axis, dim in sides:
        size, length = (lax.axis_size(axis), array.shape[dim])
        up = [(i, (i + 1) % size) for i in range(size - 1)]
        down = [(j, i) for i, j in up]
        last = lax.slice_in_dim(array, length - width, length, axis=dim)
        initial = lax.slice_in_dim(array, 0, width, axis=dim)
        before = lax.ppermute(last, axis, up)
        after = lax.ppermute(initial, axis, down)
        array = jnp.concatenate([before, array, after], axis=dim)
    return array


def release(water, convey):
    rate = convey * jnp.cbrt(water * water)
    return water * (1.0 - jnp.exp(-rate))


def collect(padded_out, padded_dirs):
    from_west = jnp.where(padded_dirs[1:-1, :-2] == 0, padded_out[1:-1, :-2], 0.0)
    from_east = jnp.where(padded_dirs[1:-1, 2:] == 1, padded_out[1:-1, 2:], 0.0)
    from_north = jnp.where(padded_dirs[:-2, 1:-1] == 2, padded_out[:-2, 1:-1], 0.0)
    from_south = jnp.where(padded_dirs[2:, 1:-1] == 3, padded_out[2:, 1:-1], 0.0)
    return from_west + from_east + from_north + from_south


def lagged(flows):
    one_back = jnp.pad(flows, ((0, 0), (1, 0)))[:, :-1]
    two_back = jnp.pad(flows, ((0, 0), (2, 0)))[:, :-2]
    return RECENT * one_back + EARLIER * two_back


def exact_dot(left, right):
    return jnp.dot(left, right, precision=EXACT, preferred_element_type=jnp.float32)


def local(
    depth_start,
    conveyance,
    cell_rain,
    nitrogen,
    flow_dir,
    unit_hydro,
    rain_hours,
    send_rows,
    send_owner,
    send_down,
):
    nitrogen_left = nitrogen
    margin = STEPS
    stacked = jnp.stack([depth_start, conveyance, cell_rain])
    extended = extended_2(stacked, (("wide", 1), ("narrow", 2)), margin)
    wide_dirs = extended_2(flow_dir, (("wide", 0), ("narrow", 1)), margin)
    water_ext = extended[0]
    convey_ext = extended[1]
    rain_ext = extended[2]
    padded_dirs = jnp.pad(wide_dirs, 1)
    for step_index in range(STEPS):
        outflow = release(water_ext, convey_ext)
        water_ext = water_ext - outflow + collect(jnp.pad(outflow, 1), padded_dirs) + rain_ext
        inner_out = outflow[margin:-margin, margin:-margin]
        nitrogen_left = nitrogen_left - nitrogen_left * (1.0 - jnp.exp(-WASH * inner_out))
    water = water_ext[margin:-margin, margin:-margin]
    tile_rows = water.shape[0]
    tile_cols = water.shape[1]
    yields = jnp.mean(
        water.reshape(tile_rows // SUB_ROWS, SUB_ROWS, tile_cols // SUB_COLS, SUB_COLS), axis=(1, 3)
    ).reshape(-1)
    hour_count = unit_hydro.shape[0]
    kernel = unit_hydro.astype(jnp.bfloat16)
    pattern = jnp.concatenate([kernel, jnp.zeros((hour_count,), jnp.bfloat16)])
    repeated = jnp.tile(pattern, hour_count)[: hour_count * (2 * hour_count - 1)]
    toeplitz = repeated.reshape(hour_count, 2 * hour_count - 1)[:, :hour_count]
    excess = (rain_hours[0].astype(jnp.float32) * yields[:, None]).astype(jnp.bfloat16)
    flows_total = jnp.dot(excess, toeplitz, preferred_element_type=jnp.float32)
    sub_count = flows_total.shape[0]
    owners = lax.axis_size("wide")
    capacity = sub_count // 128
    owner_ids = jnp.arange(owners, dtype=jnp.int32)
    sub_iota = jnp.arange(sub_count, dtype=jnp.int32)
    list_len = send_rows.shape[3]
    list_iota = jnp.arange(list_len, dtype=jnp.int32)
    earlier = (list_iota[None, :] < list_iota[:, None]).astype(jnp.float32)
    slot_iota = jnp.arange(owners * capacity, dtype=jnp.int32)
    for level_index in range(send_rows.shape[1]):
        rows_level = send_rows[0, level_index, 0]
        owner_level = send_owner[0, level_index, 0]
        down_level = send_down[0, level_index, 0]
        is_valid = (rows_level >= 0) & (owner_level >= 0) & (down_level >= 0)
        picker = ((rows_level[:, None] == sub_iota[None, :]) & is_valid[:, None]).astype(
            jnp.float32
        )
        routed = lagged(exact_dot(picker, flows_total))
        onehot = ((owner_level[:, None] == owner_ids[None, :]) & is_valid[:, None]).astype(
            jnp.float32
        )
        before = exact_dot(earlier, onehot)
        position = jnp.sum(before * onehot, axis=1).astype(jnp.int32)
        slot_index = jnp.where(is_valid, owner_level * capacity + position, owners * capacity)
        placer = (slot_index[None, :] == slot_iota[:, None]).astype(jnp.float32)
        outgoing = exact_dot(placer, routed)
        shifted_down = (down_level + 1).astype(jnp.float32)
        target_rows = jnp.sum(placer * shifted_down[None, :], axis=1).astype(jnp.int32) - 1
        incoming, arrived_rows = (
            lax.all_to_all(
                outgoing.reshape(owners, capacity, hour_count),
                "wide",
                split_axis=0,
                concat_axis=0,
                tiled=True,
            ),
            lax.all_to_all(
                target_rows.reshape(owners, capacity),
                "wide",
                split_axis=0,
                concat_axis=0,
                tiled=True,
            ),
        )
        flat_rows = arrived_rows.reshape(-1)
        receiver = (flat_rows[None, :] == sub_iota[:, None]).astype(jnp.float32)
        flows_total = flows_total + exact_dot(receiver, incoming.reshape(-1, hour_count))
    return (water, nitrogen_left, flows_total[None])


def solution(mesh):
    placed = (
        P("wide", "narrow"),
        P("wide", "narrow"),
        P("wide", "narrow"),
        P("wide", "narrow"),
        P("wide", "narrow"),
        P(),
        P("narrow", "wide", None),
        P("narrow", None, "wide", None),
        P("narrow", None, "wide", None),
        P("narrow", None, "wide", None),
    )
    return jax.shard_map(
        local,
        mesh=mesh,
        in_specs=placed,
        out_specs=(P("wide", "narrow"), P("wide", "narrow"), P("narrow", "wide", None)),
        check_vma=False,
    )
```

profile of v0, /device:TPU:0, one launch (start us, length us, event | category | flops | bytes accessed | tf_op | source)
XLA Modules:
  0.0 208.8 jit_solution(2129510482665130499)
XLA Ops:
  2.9 4.5 %collective-permute-start = (f32[3,4,512]{2,1,0:T(4,128)S(1)}, f32[3,4,512]{2,1,0:T(4,128)S(1)}, u32[]{:S(2)}, u32[]{:S(2)}) collective-permute-start(f32[3,4,512]{2,1,0:T(4,128)S(1)} %get-tuple-element.15), channel_id=1, source_target_pairs={{0,8},{8,16},{16,24},{24,32},{32,40},{40,48},{48,56},{56,64},{64,7... | collective-permute-start | bytes 73736 | tf_op jit(solution)/shard_map/ppermute | solution.py:24
  9.4 4.5 %collective-permute-start.4 = (s32[4,512]{1,0:T(4,128)S(1)}, s32[4,512]{1,0:T(4,128)S(1)}, u32[]{:S(2)}, u32[]{:S(2)}) collective-permute-start(s32[4,512]{1,0:T(4,128)S(1)} %get-tuple-element.25), channel_id=1, source_target_pairs={{0,8},{8,16},{16,24},{24,32},{32,40},{40,48},{48,56},{56,64},{64,7... | collective-permute-start | bytes 24584 | tf_op jit(solution)/shard_map/ppermute | solution.py:24
  18.7 11.8 %all-to-all-start = ((s32[16,1,16]{2,1,0:T(1,128)}), s32[16,1,16]{2,1,0:T(1,128)S(1)}, u32[]{:S(2)}, u32[]{:S(2)}) async-start(s32[16,1,16]{2,1,0:T(1,128)} %sub.90), calls=%async_computation | async-start | bytes 16384 | tf_op jit(solution)/shard_map/all_to_all | solution.py:128
  35.5 3.0 %collective-permute-start.6 = (s32[136,4]{1,0:T(8,128)S(1)}, s32[136,4]{1,0:T(8,128)S(1)}, u32[]{:S(2)}, u32[]{:S(2)}) collective-permute-start(s32[136,4]{1,0:T(8,128)S(1)} %get-tuple-element.23), channel_id=1, source_target_pairs={{0,1},{1,2},{2,3},{3,4},{4,5},{5,6},{6,7},{8,9},{9,10},{10,11},{11... | collective-permute-start | bytes 6536 | tf_op jit(solution)/shard_map/ppermute | solution.py:24
  40.0 3.9 %collective-permute-start.2 = (f32[3,136,4]{2,1,0:T(8,128)S(1)}, f32[3,136,4]{2,1,0:T(8,128)S(1)}, u32[]{:S(2)}, u32[]{:S(2)}) collective-permute-start(f32[3,136,4]{2,1,0:T(8,128)S(1)} %get-tuple-element.13), channel_id=1, source_target_pairs={{0,1},{1,2},{2,3},{3,4},{4,5},{5,6},{6,7},{8,9},{9,10},{10,11},{11... | collective-permute-start | bytes 19592 | tf_op jit(solution)/shard_map/ppermute | solution.py:24
  48.2 2.0 multiply_subtract_fusion
  51.3 2.9 %fusion.1 = f32[2048,512]{1,0:T(8,128)S(1)} fusion(bf16[1,2048,512]{2,1,0:T(8,128)(2,1)} %param.16, f32[2048]{0:T(1024)S(1)} %div.10, bf16[512,1023]{1,0:T(8,128)(2,1)S(1)} %reshape.443), kind=kOutput, calls=%fused_computation.7 | convolution fusion | flops 1076887552 | bytes 6823936 | tf_op jit(solution)/shard_map/dot_general | solution.py:91
  54.2 2.0 copy-done
  59.2 7.2 %all-to-all-start.1 = ((f32[16,16,512]{2,1,0:T(8,128)}), f32[16,16,512]{2,1,0:T(8,128)S(1)}, u32[]{:S(2)}, u32[]{:S(2)}) async-start(f32[16,16,512]{2,1,0:T(8,128)} %bitcast.11), calls=%async_computation.1 | async-start | bytes 1048576 | tf_op jit(solution)/shard_map/all_to_all | solution.py:121
  68.4 9.3 %all-to-all-done.1 = f32[16,16,512]{2,1,0:T(8,128)S(1)} async-done(((f32[16,16,512]{2,1,0:T(8,128)}), f32[16,16,512]{2,1,0:T(8,128)S(1)}, u32[]{:S(2)}, u32[]{:S(2)}) %all-to-all-start.1) | async-done | bytes 524320 | tf_op jit(solution)/shard_map/all_to_all | solution.py:121
  77.7 3.7 %all-to-all-start.2 = ((s32[16,1,16]{2,1,0:T(1,128)}), s32[16,1,16]{2,1,0:T(1,128)S(1)}, u32[]{:S(2)}, u32[]{:S(2)}) async-start(s32[16,1,16]{2,1,0:T(1,128)} %sub.92), calls=%async_computation.2 | async-start | bytes 16384 | tf_op jit(solution)/shard_map/all_to_all | solution.py:128
  81.4 4.3 %convolution_add_fusion.3 = f32[2048,512]{1,0:T(8,128)S(1)} fusion(f32[2048,512]{1,0:T(8,128)} %copy-done, f32[256,512]{1,0:T(8,128)S(1)} %bitcast.143, s32[256]{0:T(256)S(1)} %eq.148), kind=kOutput, calls=%fused_computation.6 | convolution fusion | flops 3222798336 | bytes 8913920 | tf_op jit(solution)/shard_map/dot_general | solution.py:50
  85.7 2.0 copy-done.2
  87.7 1.7 fusion.19
  90.7 6.9 %all-to-all-start.3 = ((f32[16,16,512]{2,1,0:T(8,128)}), f32[16,16,512]{2,1,0:T(8,128)S(1)}, u32[]{:S(2)}, u32[]{:S(2)}) async-start(f32[16,16,512]{2,1,0:T(8,128)} %bitcast.17), calls=%async_computation.3 | async-start | bytes 1048576 | tf_op jit(solution)/shard_map/all_to_all | solution.py:121
  99.2 11.8 %all-to-all-done.3 = f32[16,16,512]{2,1,0:T(8,128)S(1)} async-done(((f32[16,16,512]{2,1,0:T(8,128)}), f32[16,16,512]{2,1,0:T(8,128)S(1)}, u32[]{:S(2)}, u32[]{:S(2)}) %all-to-all-start.3) | async-done | bytes 524320 | tf_op jit(solution)/shard_map/all_to_all | solution.py:121
  111.0 3.5 %all-to-all-start.4 = ((s32[16,1,16]{2,1,0:T(1,128)}), s32[16,1,16]{2,1,0:T(1,128)S(1)}, u32[]{:S(2)}, u32[]{:S(2)}) async-start(s32[16,1,16]{2,1,0:T(1,128)} %sub.94), calls=%async_computation.4 | async-start | bytes 16384 | tf_op jit(solution)/shard_map/all_to_all | solution.py:128
  114.5 4.3 %convolution_add_fusion.2 = f32[2048,512]{1,0:T(8,128)S(1)} fusion(f32[2048,512]{1,0:T(8,128)} %copy-done.2, f32[256,512]{1,0:T(8,128)S(1)} %bitcast.145, s32[256]{0:T(256)S(1)} %eq.317), kind=kOutput, calls=%fused_computation.5 | convolution fusion | flops 3222798336 | bytes 8913920 | tf_op jit(solution)/shard_map/dot_general | solution.py:50
  118.8 2.0 copy-done.3
  123.8 7.1 %all-to-all-start.5 = ((f32[16,16,512]{2,1,0:T(8,128)}), f32[16,16,512]{2,1,0:T(8,128)S(1)}, u32[]{:S(2)}, u32[]{:S(2)}) async-start(f32[16,16,512]{2,1,0:T(8,128)} %bitcast.23), calls=%async_computation.5 | async-start | bytes 1048576 | tf_op jit(solution)/shard_map/all_to_all | solution.py:121
  132.5 10.0 %all-to-all-done.5 = f32[16,16,512]{2,1,0:T(8,128)S(1)} async-done(((f32[16,16,512]{2,1,0:T(8,128)}), f32[16,16,512]{2,1,0:T(8,128)S(1)}, u32[]{:S(2)}, u32[]{:S(2)}) %all-to-all-start.5) | async-done | bytes 524320 | tf_op jit(solution)/shard_map/all_to_all | solution.py:121
  142.5 3.7 %all-to-all-start.6 = ((s32[16,1,16]{2,1,0:T(1,128)}), s32[16,1,16]{2,1,0:T(1,128)S(1)}, u32[]{:S(2)}, u32[]{:S(2)}) async-start(s32[16,1,16]{2,1,0:T(1,128)} %sub.96), calls=%async_computation.6 | async-start | bytes 16384 | tf_op jit(solution)/shard_map/all_to_all | solution.py:128
  146.3 4.3 %convolution_add_fusion.1 = f32[2048,512]{1,0:T(8,128)S(1)} fusion(f32[2048,512]{1,0:T(8,128)} %copy-done.3, f32[256,512]{1,0:T(8,128)S(1)} %bitcast.146, s32[256]{0:T(256)S(1)} %eq.330), kind=kOutput, calls=%fused_computation.4 | convolution fusion | flops 3222798336 | bytes 8913920 | tf_op jit(solution)/shard_map/dot_general | solution.py:50
  150.6 2.0 copy-done.1
  155.6 6.9 %all-to-all-start.7 = ((f32[16,16,512]{2,1,0:T(8,128)}), f32[16,16,512]{2,1,0:T(8,128)S(1)}, u32[]{:S(2)}, u32[]{:S(2)}) async-start(f32[16,16,512]{2,1,0:T(8,128)} %bitcast.29), calls=%async_computation.7 | async-start | bytes 1048576 | tf_op jit(solution)/shard_map/all_to_all | solution.py:121
  164.0 8.6 %all-to-all-done.7 = f32[16,16,512]{2,1,0:T(8,128)S(1)} async-done(((f32[16,16,512]{2,1,0:T(8,128)}), f32[16,16,512]{2,1,0:T(8,128)S(1)}, u32[]{:S(2)}, u32[]{:S(2)}) %all-to-all-start.7) | async-done | bytes 524320 | tf_op jit(solution)/shard_map/all_to_all | solution.py:121
  172.6 3.5 %all-to-all-start.8 = ((s32[16,1,16]{2,1,0:T(1,128)}), s32[16,1,16]{2,1,0:T(1,128)S(1)}, u32[]{:S(2)}, u32[]{:S(2)}) async-start(s32[16,1,16]{2,1,0:T(1,128)} %sub.98), calls=%async_computation.8 | async-start | bytes 16384 | tf_op jit(solution)/shard_map/all_to_all | solution.py:128
  176.1 4.3 %convolution_add_fusion = f32[2048,512]{1,0:T(8,128)S(1)} fusion(f32[2048,512]{1,0:T(8,128)} %copy-done.1, f32[256,512]{1,0:T(8,128)S(1)} %bitcast.144, s32[256]{0:T(256)S(1)} %eq.343), kind=kOutput, calls=%fused_computation.3 | convolution fusion | flops 3222798336 | bytes 8913920 | tf_op jit(solution)/shard_map/dot_general | solution.py:50
  180.4 2.0 copy-done.4
  185.4 7.1 %all-to-all-start.9 = ((f32[16,16,512]{2,1,0:T(8,128)}), f32[16,16,512]{2,1,0:T(8,128)S(1)}, u32[]{:S(2)}, u32[]{:S(2)}) async-start(f32[16,16,512]{2,1,0:T(8,128)} %bitcast.35), calls=%async_computation.9 | async-start | bytes 1048576 | tf_op jit(solution)/shard_map/all_to_all | solution.py:121
  193.2 9.5 %all-to-all-done.9 = f32[16,16,512]{2,1,0:T(8,128)S(1)} async-done(((f32[16,16,512]{2,1,0:T(8,128)}), f32[16,16,512]{2,1,0:T(8,128)S(1)}, u32[]{:S(2)}, u32[]{:S(2)}) %all-to-all-start.9) | async-done | bytes 524320 | tf_op jit(solution)/shard_map/all_to_all | solution.py:121
  202.7 6.1 %add_bitcast_fusion = f32[1,2048,512]{2,1,0:T(8,128)} fusion(f32[2048,512]{1,0:T(8,128)} %copy-done.4, f32[256,512]{1,0:T(8,128)S(1)} %bitcast.147, s32[256]{0:T(256)S(1)} %eq.356), kind=kOutput, calls=%fused_computation.2 | convolution fusion | flops 3222798336 | bytes 8913920 | tf_op jit(solution)/shard_map/dot_general | solution.py:50
  (100 shorter events, 41.0 us)
Async XLA Ops:
  0.6 37.9 %copy-start.5 = (f32[128,512]{1,0:T(8,128)S(1)}, f32[128,512]{1,0:T(8,128)}, u32[]{:S(2)}) copy-start(f32[128,512]{1,0:T(8,128)} %param.12) | copy-start | bytes 786436
  0.6 37.9 %copy-start.6 = (f32[128,512]{1,0:T(8,128)S(1)}, f32[128,512]{1,0:T(8,128)}, u32[]{:S(2)}) copy-start(f32[128,512]{1,0:T(8,128)} %param.11) | copy-start | bytes 786436
  0.7 37.9 %copy-start.7 = (f32[128,512]{1,0:T(8,128)S(1)}, f32[128,512]{1,0:T(8,128)}, u32[]{:S(2)}) copy-start(f32[128,512]{1,0:T(8,128)} %param.10) | copy-start | bytes 786436
  0.7 33.4 %copy-start.8 = (s32[128,512]{1,0:T(8,128)S(1)}, s32[128,512]{1,0:T(8,128)}, u32[]{:S(2)}) copy-start(s32[128,512]{1,0:T(8,128)} %param.14) | copy-start | bytes 786436
  1.6 37.0 %collective-permute-start.1 = (f32[3,4,512]{2,1,0:T(4,128)S(1)}, f32[3,4,512]{2,1,0:T(4,128)S(1)}, u32[]{:S(2)}, u32[]{:S(2)}) collective-permute-start(f32[3,4,512]{2,1,0:T(4,128)S(1)} %get-tuple-element.16), channel_id=1, source_target_pairs={{8,0},{16,8},{24,16},{32,24},{40,32},{48,40},{56,48},{64,56},{72,6... | collective-permute-start | bytes 73736 | tf_op jit(solution)/shard_map/ppermute | solution.py:25
  2.9 35.7 %collective-permute-start = (f32[3,4,512]{2,1,0:T(4,128)S(1)}, f32[3,4,512]{2,1,0:T(4,128)S(1)}, u32[]{:S(2)}, u32[]{:S(2)}) collective-permute-start(f32[3,4,512]{2,1,0:T(4,128)S(1)} %get-tuple-element.15), channel_id=1, source_target_pairs={{0,8},{8,16},{16,24},{24,32},{32,40},{40,48},{48,56},{56,64},{64,7... | collective-permute-start | bytes 73736 | tf_op jit(solution)/shard_map/ppermute | solution.py:24
  8.2 25.9 %collective-permute-start.5 = (s32[4,512]{1,0:T(4,128)S(1)}, s32[4,512]{1,0:T(4,128)S(1)}, u32[]{:S(2)}, u32[]{:S(2)}) collective-permute-start(s32[4,512]{1,0:T(4,128)S(1)} %get-tuple-element.26), channel_id=1, source_target_pairs={{8,0},{16,8},{24,16},{32,24},{40,32},{48,40},{56,48},{64,56},{72,6... | collective-permute-start | bytes 24584 | tf_op jit(solution)/shard_map/ppermute | solution.py:25
  9.4 24.6 %collective-permute-start.4 = (s32[4,512]{1,0:T(4,128)S(1)}, s32[4,512]{1,0:T(4,128)S(1)}, u32[]{:S(2)}, u32[]{:S(2)}) collective-permute-start(s32[4,512]{1,0:T(4,128)S(1)} %get-tuple-element.25), channel_id=1, source_target_pairs={{0,8},{8,16},{16,24},{24,32},{32,40},{40,48},{48,56},{56,64},{64,7... | collective-permute-start | bytes 24584 | tf_op jit(solution)/shard_map/ppermute | solution.py:24
  18.7 40.6 %all-to-all-start = ((s32[16,1,16]{2,1,0:T(1,128)}), s32[16,1,16]{2,1,0:T(1,128)S(1)}, u32[]{:S(2)}, u32[]{:S(2)}) async-start(s32[16,1,16]{2,1,0:T(1,128)} %sub.90), calls=%async_computation | async-start | bytes 16384 | tf_op jit(solution)/shard_map/all_to_all | solution.py:128
  34.2 9.8 %collective-permute-start.7 = (s32[136,4]{1,0:T(8,128)S(1)}, s32[136,4]{1,0:T(8,128)S(1)}, u32[]{:S(2)}, u32[]{:S(2)}) collective-permute-start(s32[136,4]{1,0:T(8,128)S(1)} %get-tuple-element.24), channel_id=1, source_target_pairs={{1,0},{2,1},{3,2},{4,3},{5,4},{6,5},{7,6},{9,8},{10,9},{11,10},{12... | collective-permute-start | bytes 6536 | tf_op jit(solution)/shard_map/ppermute | solution.py:25
  35.5 8.5 %collective-permute-start.6 = (s32[136,4]{1,0:T(8,128)S(1)}, s32[136,4]{1,0:T(8,128)S(1)}, u32[]{:S(2)}, u32[]{:S(2)}) collective-permute-start(s32[136,4]{1,0:T(8,128)S(1)} %get-tuple-element.23), channel_id=1, source_target_pairs={{0,1},{1,2},{2,3},{3,4},{4,5},{5,6},{6,7},{8,9},{9,10},{10,11},{11... | collective-permute-start | bytes 6536 | tf_op jit(solution)/shard_map/ppermute | solution.py:24
  38.7 5.4 %collective-permute-start.3 = (f32[3,136,4]{2,1,0:T(8,128)S(1)}, f32[3,136,4]{2,1,0:T(8,128)S(1)}, u32[]{:S(2)}, u32[]{:S(2)}) collective-permute-start(f32[3,136,4]{2,1,0:T(8,128)S(1)} %get-tuple-element.14), channel_id=1, source_target_pairs={{1,0},{2,1},{3,2},{4,3},{5,4},{6,5},{7,6},{9,8},{10,9},{11,10},{12... | collective-permute-start | bytes 19592 | tf_op jit(solution)/shard_map/ppermute | solution.py:25
  40.0 4.8 %collective-permute-start.2 = (f32[3,136,4]{2,1,0:T(8,128)S(1)}, f32[3,136,4]{2,1,0:T(8,128)S(1)}, u32[]{:S(2)}, u32[]{:S(2)}) collective-permute-start(f32[3,136,4]{2,1,0:T(8,128)S(1)} %get-tuple-element.13), channel_id=1, source_target_pairs={{0,1},{1,2},{2,3},{3,4},{4,5},{5,6},{6,7},{8,9},{9,10},{10,11},{11... | collective-permute-start | bytes 19592 | tf_op jit(solution)/shard_map/ppermute | solution.py:24
  45.6 2.5 %copy-start.10 = (f32[128,512]{1,0:T(8,128)S(1)}, f32[128,512]{1,0:T(8,128)}, u32[]{:S(2)}) copy-start(f32[128,512]{1,0:T(8,128)} %param.13) | copy-start | bytes 786436
  50.1 4.1 %copy-start.9 = (f32[128,512]{1,0:T(8,128)}, f32[128,512]{1,0:T(8,128)S(1)}, u32[]{:S(2)}) copy-start(f32[128,512]{1,0:T(8,128)S(1)} %get-tuple-element.18) | copy-start | bytes 786436
  54.2 2.0 copy-start
  59.2 18.5 %all-to-all-start.1 = ((f32[16,16,512]{2,1,0:T(8,128)}), f32[16,16,512]{2,1,0:T(8,128)S(1)}, u32[]{:S(2)}, u32[]{:S(2)}) async-start(f32[16,16,512]{2,1,0:T(8,128)} %bitcast.11), calls=%async_computation.1 | async-start | bytes 1048576 | tf_op jit(solution)/shard_map/all_to_all | solution.py:121
  77.7 13.0 %all-to-all-start.2 = ((s32[16,1,16]{2,1,0:T(1,128)}), s32[16,1,16]{2,1,0:T(1,128)S(1)}, u32[]{:S(2)}, u32[]{:S(2)}) async-start(s32[16,1,16]{2,1,0:T(1,128)} %sub.92), calls=%async_computation.2 | async-start | bytes 16384 | tf_op jit(solution)/shard_map/all_to_all | solution.py:128
  85.7 2.0 copy-start.2
  90.7 20.3 %all-to-all-start.3 = ((f32[16,16,512]{2,1,0:T(8,128)}), f32[16,16,512]{2,1,0:T(8,128)S(1)}, u32[]{:S(2)}, u32[]{:S(2)}) async-start(f32[16,16,512]{2,1,0:T(8,128)} %bitcast.17), calls=%async_computation.3 | async-start | bytes 1048576 | tf_op jit(solution)/shard_map/all_to_all | solution.py:121
  111.0 12.8 %all-to-all-start.4 = ((s32[16,1,16]{2,1,0:T(1,128)}), s32[16,1,16]{2,1,0:T(1,128)S(1)}, u32[]{:S(2)}, u32[]{:S(2)}) async-start(s32[16,1,16]{2,1,0:T(1,128)} %sub.94), calls=%async_computation.4 | async-start | bytes 16384 | tf_op jit(solution)/shard_map/all_to_all | solution.py:128
  118.8 2.0 copy-start.3
  123.8 18.7 %all-to-all-start.5 = ((f32[16,16,512]{2,1,0:T(8,128)}), f32[16,16,512]{2,1,0:T(8,128)S(1)}, u32[]{:S(2)}, u32[]{:S(2)}) async-start(f32[16,16,512]{2,1,0:T(8,128)} %bitcast.23), calls=%async_computation.5 | async-start | bytes 1048576 | tf_op jit(solution)/shard_map/all_to_all | solution.py:121
  142.5 13.1 %all-to-all-start.6 = ((s32[16,1,16]{2,1,0:T(1,128)}), s32[16,1,16]{2,1,0:T(1,128)S(1)}, u32[]{:S(2)}, u32[]{:S(2)}) async-start(s32[16,1,16]{2,1,0:T(1,128)} %sub.96), calls=%async_computation.6 | async-start | bytes 16384 | tf_op jit(solution)/shard_map/all_to_all | solution.py:128
  150.6 2.0 copy-start.1
  155.6 17.0 %all-to-all-start.7 = ((f32[16,16,512]{2,1,0:T(8,128)}), f32[16,16,512]{2,1,0:T(8,128)S(1)}, u32[]{:S(2)}, u32[]{:S(2)}) async-start(f32[16,16,512]{2,1,0:T(8,128)} %bitcast.29), calls=%async_computation.7 | async-start | bytes 1048576 | tf_op jit(solution)/shard_map/all_to_all | solution.py:121
  172.6 12.8 %all-to-all-start.8 = ((s32[16,1,16]{2,1,0:T(1,128)}), s32[16,1,16]{2,1,0:T(1,128)S(1)}, u32[]{:S(2)}, u32[]{:S(2)}) async-start(s32[16,1,16]{2,1,0:T(1,128)} %sub.98), calls=%async_computation.8 | async-start | bytes 16384 | tf_op jit(solution)/shard_map/all_to_all | solution.py:128
  180.4 2.0 copy-start.4
  185.4 17.3 %all-to-all-start.9 = ((f32[16,16,512]{2,1,0:T(8,128)}), f32[16,16,512]{2,1,0:T(8,128)S(1)}, u32[]{:S(2)}, u32[]{:S(2)}) async-start(f32[16,16,512]{2,1,0:T(8,128)} %bitcast.35), calls=%async_computation.9 | async-start | bytes 1048576 | tf_op jit(solution)/shard_map/all_to_all | solution.py:121
where the time goes:
time: 210 us; the launch traced here: 209 us
  starting transfers between devices  82.7 us (39%)
  waiting for transfers between devices  49.9 us (24%)
  matrix products  42 us (20%)
  local copies, waits for them, and re-layouts  19.8 us (9%)
  other arithmetic  13.2 us (6%)
    all_to_all x5, waiting for transfers between devices, local(): lax.all_to_all(outgoing.reshape(owners, capacity, hour_count), 'wide', sp...  49.2 us
    dot_general x20, matrix products, exact_dot(): jnp.dot(left, right, precision=EXACT, preferred_element_type=jnp.float32)  39.1 us
    all_to_all x5, starting transfers between devices, local(): lax.all_to_all(outgoing.reshape(owners, capacity, hour_count), 'wide', sp...  35.3 us
    all_to_all x5, starting transfers between devices, local(): lax.all_to_all(target_rows.reshape(owners, capacity), 'wide', split_axis=...  26.2 us
    ppermute x4, starting transfers between devices, extended_2(): before = lax.ppermute(last, axis, up)  16 us
    unnamed x24, local copies, waits for them, and re-layouts  10.6 us
    ppermute x4, starting transfers between devices, extended_2(): after = lax.ppermute(initial, axis, down)  5.16 us
  transfers between devices with their start and end apart: 18, of which 6 were waited for; matrix products, arithmetic and copies ran while one was open for 28% of the time, Pallas kernels for 0%

commit v1 on v0

v1 whole, which is shorter than its diff:
```python
import functools
import jax
import jax.numpy as jnp
from jax import lax
from jax.experimental import pallas as pl
from jax.experimental.pallas import tpu as pltpu
from jax.sharding import PartitionSpec as P

SUB_ROWS = 2
SUB_COLS = 16
STEPS = 4
WASH = 1.5
RECENT = 0.6
EARLIER = 0.3
EXACT = lax.Precision.HIGHEST

OWN = 16
LEV = 5
LIST = 128
SUBS = 2048
HRS = 512
ROWS = 128
COLS = 512
HOPS = LEV
ENT = LEV * LIST

SLOTS = 96
DATA = SLOTS - 1
MULTI = 32
EXTRA = 32

F32 = jnp.float32
BF = jnp.bfloat16
I32 = jnp.int32

VM = pl.BlockSpec(memory_space=pltpu.VMEM)


def nt_dot(a, b):
    return lax.dot_general(a, b, (((1,), (1,)), ((), ())), preferred_element_type=F32)


def nn_dot(a, b):
    return lax.dot_general(a, b, (((1,), (0,)), ((), ())), preferred_element_type=F32)


def iota(shape, dim):
    return lax.broadcasted_iota(I32, shape, dim)


def entry_keys(rows_ref, owner_ref, down_ref, level):
    rows = rows_ref[0, level]
    owner = owner_ref[0, level]
    down = down_ref[0, level]
    valid = (rows >= 0) & (owner >= 0) & (down >= 0)
    return jnp.where(valid, rows, -1), jnp.where(valid, owner * SUBS + down + 1, 0)


def map_kernel(rows_ref, owner_ref, down_ref, out_ref):
    acc = jnp.zeros((2 * OWN, LIST), F32)
    for level in range(LEV):
        rows, key = entry_keys(rows_ref, owner_ref, down_ref, level)
        hi = rows >> 7
        lo = rows & 127
        at_hi = iota((OWN, LIST), 0) == hi
        upper = jnp.where(at_hi, key >> 8, 0).astype(F32)
        lower = jnp.where(at_hi, key & 255, 0).astype(F32)
        left = jnp.concatenate([upper, lower], axis=0).astype(BF)
        right = jnp.where(iota((LIST, LIST), 0) == lo, 1.0, 0.0).astype(BF)
        acc = acc + nt_dot(left, right)
    table = acc[:OWN] * 256.0 + acc[OWN:]
    for owner in range(OWN):
        out_ref[owner] = table


def plan_kernel(rows_ref, owner_ref, down_ref, full_ref, slot_ref, left_ref, meta_ref):
    full = full_ref[...].reshape(OWN * OWN, LIST).astype(I32)
    parts = jnp.concatenate([(full >> 8).astype(F32), (full & 255).astype(F32)], axis=1)
    parts_t = jnp.transpose(parts).astype(BF)
    keys = [
        jnp.concatenate(
            [entry_keys(rows_ref, owner_ref, down_ref, level)[1] for level in range(LEV)], axis=1
        )
    ]
    for hop in range(1, HOPS):
        at = keys[-1] - 1
        pick_hi = jnp.where(iota((OWN * OWN, ENT), 0) == (at >> 7), 1.0, 0.0).astype(BF)
        found = nn_dot(parts_t, pick_hi)
        value = found[:LIST] * 256.0 + found[LIST:]
        at_lo = iota((LIST, ENT), 0) == (at & 127)
        keys.append(jnp.sum(jnp.where(at_lo, value, 0.0), axis=0, keepdims=True).astype(I32))
    order = list(range(1, HOPS)) + [0]
    upper_tri = jnp.where(iota((LIST, LIST), 0) < iota((LIST, LIST), 1), 1.0, 0.0).astype(BF)

    def blocks_of(key_list):
        blocks = []
        for hop in order:
            owner = (key_list[hop] - 1) >> 11
            for level in range(LEV):
                part = owner[:, level * LIST : (level + 1) * LIST]
                blocks.append(jnp.where(iota((OWN, LIST), 0) == part, 1.0, 0.0))
        counts = nn_dot(jnp.concatenate(blocks, axis=0).astype(BF), upper_tri)
        return blocks, counts

    blocks, counts = blocks_of(keys)
    n_multi = (HOPS - 1) * LEV
    base = jnp.zeros((OWN, 1), F32)
    slots = [None] * HOPS
    pieces = []
    for index in range(HOPS * LEV):
        if index == n_multi:
            base = jnp.minimum(base, float(MULTI))
        block = blocks[index]
        count = counts[index * OWN : (index + 1) * OWN]
        pieces.append(jnp.sum(block * (count + base), axis=0, keepdims=True))
        base = base + jnp.sum(block, axis=1, keepdims=True)
    rest_keys = [None] * HOPS
    for place, hop in enumerate(order):
        rank = jnp.concatenate(pieces[place * LEV : (place + 1) * LEV], axis=1).astype(I32)
        limit = DATA if hop == 0 else MULTI
        used = keys[hop] > 0
        fits = used & (rank < limit)
        slots[hop] = jnp.where(fits, rank, -1)
        rest_keys[hop] = jnp.where(used & (rank >= limit), keys[hop], 0)
    blocks, counts = blocks_of(rest_keys)
    base = jnp.zeros((OWN, 1), F32)
    pieces = []
    for index in range(HOPS * LEV):
        block = blocks[index]
        count = counts[index * OWN : (index + 1) * OWN]
        pieces.append(jnp.sum(block * (count + base), axis=0, keepdims=True))
        base = base + jnp.sum(block, axis=1, keepdims=True)
    most_left = jnp.max(base, axis=0, keepdims=True)
    for place, hop in enumerate(order):
        rank = jnp.concatenate(pieces[place * LEV : (place + 1) * LEV], axis=1).astype(I32)
        left_ref[pl.ds(hop, 1), :] = jnp.where(rest_keys[hop] > 0, rank, -1)
        left_ref[pl.ds(8 + hop, 1), :] = rest_keys[hop]
    meta = jnp.zeros((3 * OWN, LIST), F32)
    for hop in range(HOPS):
        at = keys[hop] - 1
        owner = at >> 11
        slot_ref[pl.ds(hop, 1), :] = jnp.where(slots[hop] >= 0, owner * SLOTS + slots[hop], -1)
        goal = (at & (SUBS - 1)) + 1
        at_owner = (iota((OWN, ENT), 0) == owner) & (slots[hop] >= 0)
        left = jnp.concatenate(
            [
                jnp.where(at_owner, goal >> 4, 0).astype(F32),
                jnp.where(at_owner, goal & 15, 0).astype(F32),
                jnp.where(at_owner, float(hop + 1), 0.0),
            ],
            axis=0,
        ).astype(BF)
        right = jnp.where(iota((LIST, ENT), 0) == slots[hop], 1.0, 0.0).astype(BF)
        meta = meta + nt_dot(left, right)
    meta_ref[:, 0:128] = meta[:OWN] * 16.0 + meta[OWN : 2 * OWN]
    meta_ref[:, 128:256] = meta[2 * OWN :]
    meta_ref[:, 256:384] = jnp.broadcast_to(most_left, (OWN, 128))
    meta_ref[:, 384:512] = jnp.zeros((OWN, 128), F32)


EXT_R = 144
EXT_C = 768


def strip_kernel(d_ref, c_ref, r_ref, f_ref, north_ref, south_ref, west_ref, east_ref):
    lane = iota((ROWS, 128), 1)
    lane4 = iota((4, 128), 1)
    west_ref[...] = jnp.zeros((EXT_R, 128), F32)
    east_ref[...] = jnp.zeros((EXT_R, 128), F32)
    sides = ((west_ref, 0, 0), (east_ref, COLS - 128, 124))
    for out_ref, start, first in sides:
        body = jnp.zeros((ROWS, 128), F32)
        top = jnp.zeros((4, 128), F32)
        bottom = jnp.zeros((4, 128), F32)
        for index, ref in enumerate((d_ref, c_ref, r_ref, f_ref)):
            shift = (4 * index - first) % 128
            block = ref[:, start : start + 128]
            if index == 3:
                block = block.astype(F32)
            mine = (lane >= 4 * index) & (lane < 4 * index + 4)
            mine4 = (lane4 >= 4 * index) & (lane4 < 4 * index + 4)
            body = jnp.where(mine, roll(block, shift, 1), body)
            top = jnp.where(mine4, roll(north_ref[index, :, start : start + 128], shift, 1), top)
            bottom = jnp.where(mine4, roll(south_ref[index, :, start : start + 128], shift, 1), bottom)
        out_ref[8 : 8 + ROWS, :] = body
        out_ref[4:8, :] = top
        out_ref[8 + ROWS : 12 + ROWS, :] = bottom


def roll(x, shift, axis):
    if shift % x.shape[axis] == 0:
        return x
    return pltpu.roll(x, shift % x.shape[axis], axis)


def main_kernel(
    d_ref,
    c_ref,
    r_ref,
    f_ref,
    north_ref,
    south_ref,
    west_ref,
    east_ref,
    nitro_ref,
    hours_ref,
    rows_ref,
    slot_ref,
    meta_ref,
    water_out,
    nitro_out,
    excess_out,
    send_ref,
    w_s,
    c_s,
    r_s,
    f_s,
    o_s,
    n_s,
    u_s,
    t_s,
    picked_s,
):
    lane = iota((EXT_R, 128), 1)
    for index, (src, dst) in enumerate(((d_ref, w_s), (c_ref, c_s), (r_ref, r_s), (f_ref, f_s))):
        dst[0:8, :] = jnp.zeros((8, EXT_C), F32)
        dst[136:144, :] = jnp.zeros((8, EXT_C), F32)
        body = src[...]
        if index == 3:
            body = body.astype(F32)
        dst[8:136, 128:640] = body
        dst[4:8, 128:640] = north_ref[index]
        dst[136:140, 128:640] = south_ref[index]
        left = roll(west_ref[...], 124 - 4 * index, 1)
        dst[:, 0:128] = jnp.where(lane >= 124, left, 0.0)
        right = roll(east_ref[...], -4 * index, 1)
        dst[:, 640:768] = jnp.where(lane < 4, right, 0.0)
    t_s[...] = jnp.zeros((ROWS, COLS), F32)
    n_s[...] = jnp.zeros((EXT_R + 16, EXT_C), F32)
    u_s[...] = jnp.zeros((EXT_R + 16, EXT_C), F32)
    for step in range(STEPS):

        def first(chunk, carry):
            at = pl.multiple_of(chunk * 8, 8)
            water = w_s[pl.ds(at, 8), :]
            rate = c_s[pl.ds(at, 8), :] * jnp.exp(jnp.log(water * water) * (1.0 / 3.0))
            out = water * (1.0 - jnp.exp(-rate))
            code = f_s[pl.ds(at, 8), :]
            o_s[pl.ds(at, 8), :] = out
            n_s[pl.ds(at + 8, 8), :] = jnp.where(code == 2.0, out, 0.0)
            u_s[pl.ds(at + 8, 8), :] = jnp.where(code == 3.0, out, 0.0)
            return carry

        lax.fori_loop(0, EXT_R // 8, first, 0, unroll=2)

        for chunk in range(EXT_R // 8):
            at = chunk * 8
            out = o_s[at : at + 8, :]
            code = f_s[at : at + 8, :]
            from_west = roll(jnp.where(code == 0.0, out, 0.0), 1, 1)
            from_east = roll(jnp.where(code == 1.0, out, 0.0), -1, 1)
            from_north = n_s[at + 7 : at + 15, :]
            from_south = u_s[at + 9 : at + 17, :]
            total = from_west + from_east + from_north + from_south
            w_s[at : at + 8, :] = w_s[at : at + 8, :] - out + total + r_s[at : at + 8, :]
            if 1 <= chunk <= 16:
                t_s[at - 8 : at, :] = t_s[at - 8 : at, :] + out[:, 128:640]

    nitro_out[...] = nitro_ref[...] * jnp.exp(-WASH * t_s[...])
    water = w_s[8:136, 128:640]
    water_out[...] = water
    blocks = jnp.where(iota((32, COLS), 1) // SUB_COLS == iota((32, COLS), 0), 1.0, 0.0)
    by_row = lax.dot_general(
        blocks, water, (((1,), (1,)), ((), ())), precision=EXACT, preferred_element_type=F32
    )
    pairs = jnp.where(iota((ROWS, 128), 0) // SUB_ROWS == iota((ROWS, 128), 1), 1.0, 0.0)
    means = lax.dot_general(
        by_row, pairs, (((1,), (0,)), ((), ())), precision=EXACT, preferred_element_type=F32
    ) * (1.0 / (SUB_ROWS * SUB_COLS))
    for block in range(ROWS // SUB_ROWS):
        at = block * 32
        excess = hours_ref[0, at : at + 32, :].astype(F32) * means[:, block : block + 1]
        excess_out[at : at + 32, :] = excess.astype(BF)
    for level in range(LEV):
        pick = jnp.where(
            rows_ref[level * LIST : (level + 1) * LIST, :] == iota((LIST, SUBS), 1), 1.0, 0.0
        ).astype(BF)
        picked_s[level * LIST : (level + 1) * LIST, :] = nn_dot(pick, excess_out[...]).astype(BF)
    for owner in range(OWN):
        place = iota((SLOTS, ENT), 0) + owner * SLOTS == slot_ref[0:1, :]
        top = place[0:MULTI]
        for hop in range(1, HOPS):
            top = top | (iota((MULTI, ENT), 0) + owner * SLOTS == slot_ref[hop : hop + 1, :])
        put = jnp.concatenate([jnp.where(top, 1.0, 0.0), jnp.where(place[MULTI:], 1.0, 0.0)], axis=0)
        send_ref[owner] = nn_dot(put.astype(BF), picked_s[...])
        send_ref[owner, DATA : DATA + 1, :] = meta_ref[owner : owner + 1, :]


def lag(x):
    at = iota(x.shape, 1)
    one = jnp.where(at >= 1, roll(x, 1, 1), 0.0)
    two = jnp.where(at >= 2, roll(x, 2, 1), 0.0)
    return RECENT * one + EARLIER * two


TILE = 256


def final_kernel(recv_ref, excess_ref, kernel_ref, out_ref, high_s, low_s, goal_s, multi_s):
    @pl.when(pl.program_id(0) == 0)
    def _():
        lane = iota((8, 128), 1)
        goals = [jnp.zeros((8, 128), F32)] * (OWN * SLOTS // 128)
        multi = [jnp.zeros((8, 128), F32)] * (OWN * MULTI // 128)
        hops = []
        for src in range(OWN):
            group = recv_ref[src, DATA - 7 : DATA + 1, 0:256]
            line = jnp.broadcast_to(group[7:8, 0:128], (8, 128))
            hops.append(group[7:8, 128:256])
            for width, store in ((SLOTS, goals), (MULTI, multi)):
                start = src * width
                block, off = start // 128, start % 128
                turned = roll(line, off, 1)
                here = (lane >= off) & (lane < off + width)
                store[block] = jnp.where(here, turned, store[block])
                if off + width > 128:
                    store[block + 1] = jnp.where(lane < off + width - 128, turned, store[block + 1])
        for index, value in enumerate(goals):
            goal_s[:, index * 128 : (index + 1) * 128] = value.astype(I32) - 1
        for index, value in enumerate(multi):
            multi_s[:, index * 128 : (index + 1) * 128] = value.astype(I32) - 1
        hop_rows = jnp.concatenate(hops + [jnp.zeros((128 - OWN, 128), F32)], axis=0)
        hop_cols = jnp.transpose(hop_rows)
        for src in range(OWN):
            part = recv_ref[src, 0:MULTI, :]
            count = hop_cols[0:MULTI, src : src + 1]
            for hop in range(1, HOPS):
                part = jnp.where(count > float(hop), lag(part), part)
            high = part.astype(BF)
            high_s[src * SLOTS : src * SLOTS + MULTI, :] = high
            low_s[src * MULTI : (src + 1) * MULTI, :] = (part - high.astype(F32)).astype(BF)
            high_s[src * SLOTS + MULTI : (src + 1) * SLOTS, :] = recv_ref[src, MULTI:, :].astype(BF)

    first = pl.program_id(0) * TILE
    match = iota((TILE, OWN * SLOTS), 0) + first == goal_s[0:1, :]
    gathered = nn_dot(jnp.where(match, 1.0, 0.0).astype(BF), high_s[...])
    match = iota((TILE, OWN * MULTI), 0) + first == multi_s[0:1, :]
    gathered = gathered + nn_dot(jnp.where(match, 1.0, 0.0).astype(BF), low_s[...])
    total = excess_ref[...].astype(F32) + lag(gathered)
    high = total.astype(BF)
    low = (total - high.astype(F32)).astype(BF)
    out_ref[...] = nn_dot(high, kernel_ref[...]) + nn_dot(low, kernel_ref[...])


def neighbours(axis):
    size = lax.axis_size(axis)
    up = [(i, i + 1) for i in range(size - 1)]
    return up, [(j, i) for i, j in up]


def exchange(array):
    return lax.all_to_all(array, "wide", split_axis=0, concat_axis=0, tiled=True)


def exact_dot(left, right):
    return jnp.dot(left, right, precision=EXACT, preferred_element_type=F32)


def local(
    depth_start,
    conveyance,
    cell_rain,
    nitrogen,
    flow_dir,
    unit_hydro,
    rain_hours,
    send_rows,
    send_owner,
    send_down,
):
    table = pl.pallas_call(
        map_kernel,
        out_shape=jax.ShapeDtypeStruct((OWN, OWN, LIST), F32),
        in_specs=[VM] * 3,
        out_specs=VM,
        name="next_map",
    )(send_rows, send_owner, send_down)
    full = exchange(table)

    fields = (depth_start, conveyance, cell_rain, flow_dir)
    up, down = neighbours("wide")
    last = jnp.stack([x[-4:].astype(F32) for x in fields])
    initial = jnp.stack([x[:4].astype(F32) for x in fields])
    north = lax.ppermute(last, "wide", up)
    south = lax.ppermute(initial, "wide", down)
    west_strip, east_strip = pl.pallas_call(
        strip_kernel,
        out_shape=[jax.ShapeDtypeStruct((EXT_R, 128), F32)] * 2,
        in_specs=[VM] * 6,
        out_specs=[VM] * 2,
        name="strips",
    )(*fields, north, south)
    up, down = neighbours("narrow")
    west = lax.ppermute(east_strip, "narrow", up)
    east = lax.ppermute(west_strip, "narrow", down)

    slots, left, meta = pl.pallas_call(
        plan_kernel,
        out_shape=[
            jax.ShapeDtypeStruct((8, ENT), I32),
            jax.ShapeDtypeStruct((16, ENT), I32),
            jax.ShapeDtypeStruct((OWN, HRS), F32),
        ],
        in_specs=[VM] * 4,
        out_specs=[VM] * 3,
        name="plan",
    )(send_rows, send_owner, send_down, full)

    valid = (send_rows >= 0) & (send_owner >= 0) & (send_down >= 0)
    rows_column = jnp.where(valid, send_rows, -1).reshape(ENT, 1)
    kernel = unit_hydro.astype(BF)
    pattern = jnp.concatenate([kernel, jnp.zeros((HRS,), BF)])
    repeated = jnp.tile(pattern, HRS)[: HRS * (2 * HRS - 1)]
    toeplitz = repeated.reshape(HRS, 2 * HRS - 1)[:, :HRS]

    water, nitrogen_left, excess, outgoing = pl.pallas_call(
        main_kernel,
        out_shape=[
            jax.ShapeDtypeStruct((ROWS, COLS), F32),
            jax.ShapeDtypeStruct((ROWS, COLS), F32),
            jax.ShapeDtypeStruct((SUBS, HRS), BF),
            jax.ShapeDtypeStruct((OWN, SLOTS, HRS), F32),
        ],
        in_specs=[VM] * 13,
        out_specs=[VM] * 4,
        scratch_shapes=[pltpu.VMEM((EXT_R, EXT_C), F32)] * 5
        + [pltpu.VMEM((EXT_R + 16, EXT_C), F32)] * 2
        + [pltpu.VMEM((ROWS, COLS), F32), pltpu.VMEM((ENT, HRS), BF)],
        name="flow_and_send",
    )(*fields, north, south, west, east, nitrogen, rain_hours, rows_column, slots, meta)
    incoming = exchange(outgoing)

    discharge = pl.pallas_call(
        final_kernel,
        out_shape=jax.ShapeDtypeStruct((SUBS, HRS), F32),
        grid=(SUBS // TILE,),
        in_specs=[
            pl.BlockSpec((OWN, SLOTS, HRS), lambda i: (0, 0, 0)),
            pl.BlockSpec((TILE, HRS), lambda i: (i, 0)),
            pl.BlockSpec((HRS, HRS), lambda i: (0, 0)),
        ],
        out_specs=pl.BlockSpec((TILE, HRS), lambda i: (i, 0)),
        scratch_shapes=[
            pltpu.VMEM((OWN * SLOTS, HRS), BF),
            pltpu.VMEM((OWN * MULTI, HRS), BF),
            pltpu.VMEM((8, OWN * SLOTS), I32),
            pltpu.VMEM((8, OWN * MULTI), I32),
        ],
        name="route_and_convolve",
    )(incoming, excess, toeplitz)

    most_left = jnp.max(incoming[:, DATA, 256])
    rounds = jnp.ceil(most_left * (1.0 / EXTRA)).astype(I32)

    def more(state):
        return state[0] < rounds

    def extra_round(state):
        index, flows = state
        picker = (rows_column == jnp.arange(SUBS, dtype=I32)[None, :]).astype(F32)
        rows = exact_dot(picker, excess.astype(F32))
        slot_iota = jnp.arange(OWN * EXTRA, dtype=I32)
        send = jnp.zeros((OWN * EXTRA, HRS), F32)
        goals = jnp.zeros((OWN * EXTRA,), F32)
        for hop in range(HOPS):
            key = left[8 + hop] - 1
            rank = left[hop] - index * EXTRA
            here = (left[hop] >= 0) & (rank >= 0) & (rank < EXTRA)
            slot = jnp.where(here, (key >> 11) * EXTRA + rank, -1)
            placer = (slot[None, :] == slot_iota[:, None]).astype(F32)
            send = send + exact_dot(placer, rows)
            goals = goals + jnp.sum(placer * ((key & (SUBS - 1)) + 1).astype(F32)[None, :], axis=1)
            rows = lagged(rows)
        came = exchange(send.reshape(OWN, EXTRA, HRS)).reshape(-1, HRS)
        came_goals = exchange(goals.reshape(OWN, EXTRA)).reshape(-1).astype(I32) - 1
        routed = exact_dot(lagged(came), toeplitz.astype(F32))
        receiver = (came_goals[None, :] == jnp.arange(SUBS, dtype=I32)[:, None]).astype(F32)
        return index + 1, flows + exact_dot(receiver, routed)

    discharge = lax.while_loop(more, extra_round, (jnp.zeros((), I32), discharge))[1]
    return (water, nitrogen_left, discharge[None])


def lagged(flows):
    one_back = jnp.pad(flows, ((0, 0), (1, 0)))[:, :-1]
    two_back = jnp.pad(flows, ((0, 0), (2, 0)))[:, :-2]
    return RECENT * one_back + EARLIER * two_back


def solution(mesh):
    placed = (
        P("wide", "narrow"),
        P("wide", "narrow"),
        P("wide", "narrow"),
        P("wide", "narrow"),
        P("wide", "narrow"),
        P(),
        P("narrow", "wide", None),
        P("narrow", None, "wide", None),
        P("narrow", None, "wide", None),
        P("narrow", None, "wide", None),
    )
    return jax.shard_map(
        local,
        mesh=mesh,
        in_specs=placed,
        out_specs=(P("wide", "narrow"), P("wide", "narrow"), P("narrow", "wide", None)),
        check_vma=False,
    )
```

time: 210 us -> 129 us (0.61)
  starting transfers between devices: 82.7 us -> 21.8 us
  matrix products: 42 us -> 3.15 us
  Pallas kernels: 0 us -> 37.6 us
  local copies, waits for them, and re-layouts: 19.8 us -> 6.55 us
  other arithmetic: 13.2 us -> 2.25 us
  waiting for transfers between devices: 49.9 us -> 54.3 us
    all_to_all x10 -> x2, starting transfers between devices: 61.5 us -> 14.4 us  [exchange(): lax.all_to_all(array, 'wide', split_axis=0, concat_axis=0, tiled=True)]
    dot_general x21 -> x1, matrix products: 42 us -> 3.15 us  [exact_dot(): return jnp.dot(left, right, precision=EXACT, preferred_element_type=F32)]
    pallas_call x0 -> x5, Pallas kernels: none -> 37.6 us  [the longest x1 18.7 us: local(): pl.pallas_call(final_kernel, out_shape=jax.ShapeDtypeStruct((SUBS, HRS),...]
    ppermute x8 -> x4, starting transfers between devices: 21.2 us -> 7.37 us  [the longest x1 3.51 us: local(): north = lax.ppermute(last, 'wide', up)]
    unnamed x24 -> x20, local copies, waits for them, and re-layouts: 10.6 us -> 2.44 us
    sub x5 -> x0, local copies, waits for them, and re-layouts: 3.42 us -> none  [local(): jnp.sum(placer * shifted_down[None, :], axis=1).astype(jnp.int32) - 1]
    all_to_all x5 -> x0, other arithmetic: 2.95 us -> none  [local(): lax.all_to_all(target_rows.reshape(owners, capacity), 'wide', split_axis=...]
    mul x4 -> x0, other arithmetic: 2.58 us -> none  [release(): return water * (1.0 - jnp.exp(-rate))]
  transfers between devices with their start and end apart: 18 -> 6, of which waited for: 6 -> 3; matrix products, arithmetic and copies ran while one was open for 28% -> 5% of each run, Pallas kernels for 0% -> 4%
where the time goes in v1:
time: 129 us; the launch traced here: 127 us
  waiting for transfers between devices  54.3 us (42%)
  Pallas kernels  37.6 us (29%)
  starting transfers between devices  21.8 us (17%)
  local copies, waits for them, and re-layouts  6.55 us (5%)
  matrix products  3.15 us (2%)
  other arithmetic  2.25 us (2%)
  between operations  1.48 us (1%)
    all_to_all x2, waiting for transfers between devices, exchange(): lax.all_to_all(array, 'wide', split_axis=0, concat_axis=0, tiled=True)  51.4 us
    pallas_call x1, Pallas kernels, local(): pl.pallas_call(final_kernel, out_shape=jax.ShapeDtypeStruct((SUBS, HRS),...  18.7 us
    all_to_all x2, starting transfers between devices, exchange(): lax.all_to_all(array, 'wide', split_axis=0, concat_axis=0, tiled=True)  14.4 us
    pallas_call x1, Pallas kernels, local(): pl.pallas_call(main_kernel, out_shape=[jax.ShapeDtypeStruct((ROWS, COLS),...  11.9 us
    ppermute x1, starting transfers between devices, local(): north = lax.ppermute(last, 'wide', up)  3.51 us
    pallas_call x1, Pallas kernels, local(): pl.pallas_call(plan_kernel, out_shape=[jax.ShapeDtypeStruct((8, ENT), I32...  3.37 us
    dot_general x1, matrix products, exact_dot(): return jnp.dot(left, right, precision=EXACT, preferred_element_type=F32)  3.15 us
    ppermute x1, waiting for transfers between devices, local(): south = lax.ppermute(initial, 'wide', down)  2.89 us
  transfers between devices with their start and end apart: 6, of which 3 were waited for; matrix products, arithmetic and copies ran while one was open for 5% of the time, Pallas kernels for 4%

profile of v1, /device:TPU:0, one launch (start us, length us, event | category | flops | bytes accessed | tf_op | source)
XLA Modules:
  0.0 127.1 jit_solution(12817044150881006136)
XLA Ops:
  0.6 0.0 copy-start.6
  0.6 0.0 copy-start.7
  0.7 0.0 copy-start.5
  0.7 0.8 slice_bitcast_fusion.2
  1.4 0.7 convert_bitcast_fusion
  2.2 0.8 slice_bitcast_fusion
  2.9 3.5 %collective-permute-start = (f32[4,4,512]{2,1,0:T(4,128)S(1)}, f32[4,4,512]{2,1,0:T(4,128)S(1)}, u32[]{:S(2)}, u32[]{:S(2)}) collective-permute-start(f32[4,4,512]{2,1,0:T(4,128)S(1)} %pad_maximum_fusion), channel_id=1, source_target_pairs={{0,8},{8,16},{16,24},{24,32},{32,40},{40,48},{48,56},{56,64},{64,7... | collective-permute-start | bytes 98312 | tf_op jit(solution)/shard_map/ppermute | solution.py:394
  6.5 1.3 %collective-permute-start.1 = (f32[4,4,512]{2,1,0:T(4,128)S(1)}, f32[4,4,512]{2,1,0:T(4,128)S(1)}, u32[]{:S(2)}, u32[]{:S(2)}) collective-permute-start(f32[4,4,512]{2,1,0:T(4,128)S(1)} %pad_maximum_fusion.1), channel_id=1, source_target_pairs={{8,0},{16,8},{24,16},{32,24},{40,32},{48,40},{56,48},{64,56},{72,6... | collective-permute-start | bytes 98312 | tf_op jit(solution)/shard_map/ppermute | solution.py:395
  7.8 1.6 %next_map.1 = f32[16,16,128]{2,1,0:T(8,128)} custom-call(s32[1,5,1,128]{3,2,1,0:T(1,128)} %rows_ref.3, s32[1,5,1,128]{3,2,1,0:T(1,128)} %owner_ref.3, s32[1,5,1,128]{3,2,1,0:T(1,128)} %down_ref.3), custom_call_target="tpu_custom_call" | custom-call | tf_op jit(solution)/shard_map/next_map/pallas_call | solution.py:381
  9.4 0.0 collective-permute-done.north_ref
  9.4 2.9 %collective-permute-done.1.south_ref = f32[4,4,512]{2,1,0:T(4,128)S(1)} collective-permute-done((f32[4,4,512]{2,1,0:T(4,128)S(1)}, f32[4,4,512]{2,1,0:T(4,128)S(1)}, u32[]{:S(2)}, u32[]{:S(2)}) %collective-permute-start.1) | collective-permute-done | bytes 32800 | tf_op jit(solution)/shard_map/ppermute | solution.py:395
  12.3 0.6 copy-done.2
  12.9 2.0 %strips.1 = (f32[144,128]{1,0:T(8,128)}, f32[144,128]{1,0:T(8,128)}) custom-call(f32[128,512]{1,0:T(8,128)} %d_ref.3, f32[128,512]{1,0:T(8,128)} %c_ref.3, f32[128,512]{1,0:T(8,128)} %r_ref.3, s32[128,512]{1,0:T(8,128)} %f_ref.3, f32[4,4,512]{2,1,0:T(4,128)} %copy-done.1, f32[4,4,512]{2,1,0:T(4,128)} %copy-done.2), custom_call_target="tpu_custom_call" | custom-call | tf_op jit(solution)/shard_map/strips/pallas_call | solution.py:396
  14.9 1.3 %collective-permute-start.2 = (f32[144,128]{1,0:T(8,128)}, f32[144,128]{1,0:T(8,128)S(1)}, u32[]{:S(2)}, u32[]{:S(2)}) collective-permute-start(f32[144,128]{1,0:T(8,128)} %get-tuple-element.191), channel_id=1, source_target_pairs={{0,1},{1,2},{2,3},{3,4},{4,5},{5,6},{6,7},{8,9},{9,10},{10,11},{11... | collective-permute-start | bytes 221192 | tf_op jit(solution)/shard_map/ppermute | solution.py:404
  16.2 1.3 %collective-permute-start.3 = (f32[144,128]{1,0:T(8,128)}, f32[144,128]{1,0:T(8,128)S(1)}, u32[]{:S(2)}, u32[]{:S(2)}) collective-permute-start(f32[144,128]{1,0:T(8,128)} %get-tuple-element.192), channel_id=1, source_target_pairs={{1,0},{2,1},{3,2},{4,3},{5,4},{6,5},{7,6},{9,8},{10,9},{11,10},{12... | collective-permute-start | bytes 221192 | tf_op jit(solution)/shard_map/ppermute | solution.py:405
  17.5 9.6 %all-to-all-start.2 = ((f32[16,16,128]{2,1,0:T(8,128)}), f32[16,16,128]{2,1,0:T(8,128)S(1)}, u32[]{:S(2)}, u32[]{:S(2)}) async-start(f32[16,16,128]{2,1,0:T(8,128)} %next_map.1), calls=%async_computation.2 | async-start | bytes 262144 | tf_op jit(solution)/shard_map/all_to_all | solution.py:362
  27.2 0.9 copy.14.rows_ref
  28.1 7.0 %all-to-all-done.2.full_ref = f32[16,16,128]{2,1,0:T(8,128)S(1)} async-done(((f32[16,16,128]{2,1,0:T(8,128)}), f32[16,16,128]{2,1,0:T(8,128)S(1)}, u32[]{:S(2)}, u32[]{:S(2)}) %all-to-all-start.2) | async-done | bytes 131104 | tf_op jit(solution)/shard_map/all_to_all | solution.py:362
  35.1 0.7 copy-done
  35.8 3.4 %plan.1 = (s32[8,640]{1,0:T(8,128)}, s32[16,640]{1,0:T(8,128)S(1)}, f32[16,512]{1,0:T(8,128)}) custom-call(s32[1,5,1,128]{3,2,1,0:T(1,128)} %rows_ref.3, s32[1,5,1,128]{3,2,1,0:T(1,128)} %owner_ref.3, s32[1,5,1,128]{3,2,1,0:T(1,128)} %down_ref.3, f32[16,16,128]{2,1,0:T(8,128)} %copy-done), custom_call_target="tpu_custom_call" | custom-call | tf_op jit(solution)/shard_map/plan/pallas_call | solution.py:407
  39.2 0.0 collective-permute-done.2.west_ref
  39.2 0.6 copy-done.3
  39.8 0.0 copy-done.4
  39.8 11.9 %flow_and_send.1 = (f32[128,512]{1,0:T(8,128)}, f32[128,512]{1,0:T(8,128)}, bf16[2048,512]{1,0:T(8,128)(2,1)}, f32[16,96,512]{2,1,0:T(8,128)}) custom-call(f32[128,512]{1,0:T(8,128)} %d_ref.3, f32[128,512]{1,0:T(8,128)} %c_ref.3, f32[128,512]{1,0:T(8,128)} %r_ref.3, s32[128,512]{1,0:T(8,128)} %f_ref.3, f32[4,4,512]{2,1,0:T(4,128)} %copy-done.1, ...), custom_call_target="tpu_custom_call" | custom-call | tf_op jit(solution)/shard_map/flow_and_send/pallas_call | solution.py:426
  51.8 4.8 %all-to-all-start.3 = ((f32[16,96,512]{2,1,0:T(8,128)}), f32[16,96,512]{2,1,0:T(8,128)}, u32[]{:S(2)}, u32[]{:S(2)}) async-start(f32[16,96,512]{2,1,0:T(8,128)} %get-tuple-element.197), calls=%async_computation.3 | async-start | bytes 6291456 | tf_op jit(solution)/shard_map/all_to_all | solution.py:362
  56.6 0.2 broadcast_bitcast_fusion
  56.8 0.3 copy.15
  57.1 1.7 %reshape.131 = bf16[512,1023]{1,0:T(8,128)(2,1)S(1)} reshape(bf16[523776]{0:T(1024)(128)(2,1)S(1)} %bitcast.50) | data formatting | bytes 2095104 | tf_op jit(solution)/shard_map/reshape | solution.py:424
  58.8 3.2 %fusion.44 = f32[640,512]{1,0:T(8,128)S(1)} fusion(bf16[2048,512]{1,0:T(8,128)(2,1)} %get-tuple-element.198.excess_ref, s32[640]{0:T(1024)S(1)} %bitcast.52), kind=kOutput, calls=%fused_computation.83 | convolution fusion | flops 1343488000 | bytes 3410432 | tf_op jit(solution)/shard_map/while/body/dot_general | solution.py:366
  62.0 44.3 %all-to-all-done.3.recv_ref = f32[16,96,512]{2,1,0:T(8,128)} async-done(((f32[16,96,512]{2,1,0:T(8,128)}), f32[16,96,512]{2,1,0:T(8,128)}, u32[]{:S(2)}, u32[]{:S(2)}) %all-to-all-start.3) | async-done | bytes 3145760 | tf_op jit(solution)/shard_map/all_to_all | solution.py:362
  106.3 1.5 %slice_reduce_fusion = f32[]{:T(128)} fusion(f32[16,96,512]{2,1,0:T(8,128)} %all-to-all-done.3.recv_ref), kind=kLoop, calls=%fused_computation.89 | loop fusion | flops 15 | bytes 68 | tf_op jit(solution)/shard_map/reduce_max | solution.py:462
  108.4 18.7 %route_and_convolve.1 = f32[2048,512]{1,0:T(8,128)} custom-call(f32[16,96,512]{2,1,0:T(8,128)} %all-to-all-done.3.recv_ref, bf16[2048,512]{1,0:T(8,128)(2,1)} %get-tuple-element.198.excess_ref, bf16[512,512]{1,0:T(8,128)(2,1)S(1)} %slice.210.kernel_ref), custom_call_target="tpu_custom_call" | custom-call | tf_op jit(solution)/shard_map/route_and_convolve/pallas_call | solution.py:443
  (19 shorter events, 0.1 us)
Async XLA Ops:
  0.6 26.5 %copy-start.6 = (s32[1,5,1,128]{3,2,1,0:T(1,128)S(1)}, s32[1,5,1,128]{3,2,1,0:T(1,128)}, u32[]{:S(2)}) copy-start(s32[1,5,1,128]{3,2,1,0:T(1,128)} %down_ref.3) | copy-start | bytes 7684
  0.6 26.5 %copy-start.7 = (s32[1,5,1,128]{3,2,1,0:T(1,128)S(1)}, s32[1,5,1,128]{3,2,1,0:T(1,128)}, u32[]{:S(2)}) copy-start(s32[1,5,1,128]{3,2,1,0:T(1,128)} %owner_ref.3) | copy-start | bytes 7684
  0.7 26.5 %copy-start.5 = (s32[1,5,1,128]{3,2,1,0:T(1,128)S(1)}, s32[1,5,1,128]{3,2,1,0:T(1,128)}, u32[]{:S(2)}) copy-start(s32[1,5,1,128]{3,2,1,0:T(1,128)} %rows_ref.3) | copy-start | bytes 7684
  2.9 6.5 %collective-permute-start = (f32[4,4,512]{2,1,0:T(4,128)S(1)}, f32[4,4,512]{2,1,0:T(4,128)S(1)}, u32[]{:S(2)}, u32[]{:S(2)}) collective-permute-start(f32[4,4,512]{2,1,0:T(4,128)S(1)} %pad_maximum_fusion), channel_id=1, source_target_pairs={{0,8},{8,16},{16,24},{24,32},{32,40},{40,48},{48,56},{56,64},{64,7... | collective-permute-start | bytes 98312 | tf_op jit(solution)/shard_map/ppermute | solution.py:394
  6.5 5.8 %collective-permute-start.1 = (f32[4,4,512]{2,1,0:T(4,128)S(1)}, f32[4,4,512]{2,1,0:T(4,128)S(1)}, u32[]{:S(2)}, u32[]{:S(2)}) collective-permute-start(f32[4,4,512]{2,1,0:T(4,128)S(1)} %pad_maximum_fusion.1), channel_id=1, source_target_pairs={{8,0},{16,8},{24,16},{32,24},{40,32},{48,40},{56,48},{64,56},{72,6... | collective-permute-start | bytes 98312 | tf_op jit(solution)/shard_map/ppermute | solution.py:395
  9.4 2.9 %copy-start.1 = (f32[4,4,512]{2,1,0:T(4,128)}, f32[4,4,512]{2,1,0:T(4,128)S(1)}, u32[]{:S(2)}) copy-start(f32[4,4,512]{2,1,0:T(4,128)S(1)} %collective-permute-done.north_ref) | copy-start | bytes 98308
  12.3 0.6 copy-start.2
  14.9 24.2 %collective-permute-start.2 = (f32[144,128]{1,0:T(8,128)}, f32[144,128]{1,0:T(8,128)S(1)}, u32[]{:S(2)}, u32[]{:S(2)}) collective-permute-start(f32[144,128]{1,0:T(8,128)} %get-tuple-element.191), channel_id=1, source_target_pairs={{0,1},{1,2},{2,3},{3,4},{4,5},{5,6},{6,7},{8,9},{9,10},{10,11},{11... | collective-permute-start | bytes 221192 | tf_op jit(solution)/shard_map/ppermute | solution.py:404
  16.2 23.0 %collective-permute-start.3 = (f32[144,128]{1,0:T(8,128)}, f32[144,128]{1,0:T(8,128)S(1)}, u32[]{:S(2)}, u32[]{:S(2)}) collective-permute-start(f32[144,128]{1,0:T(8,128)} %get-tuple-element.192), channel_id=1, source_target_pairs={{1,0},{2,1},{3,2},{4,3},{5,4},{6,5},{7,6},{9,8},{10,9},{11,10},{12... | collective-permute-start | bytes 221192 | tf_op jit(solution)/shard_map/ppermute | solution.py:405
  17.5 17.6 %all-to-all-start.2 = ((f32[16,16,128]{2,1,0:T(8,128)}), f32[16,16,128]{2,1,0:T(8,128)S(1)}, u32[]{:S(2)}, u32[]{:S(2)}) async-start(f32[16,16,128]{2,1,0:T(8,128)} %next_map.1), calls=%async_computation.2 | async-start | bytes 262144 | tf_op jit(solution)/shard_map/all_to_all | solution.py:362
  35.1 0.7 copy-start
  39.2 0.6 copy-start.3
  39.2 0.6 copy-start.4
  51.8 4.8 %copy-start.8 = (f32[512]{0:T(512)S(1)}, f32[512]{0:T(512)}, u32[]{:S(2)}) copy-start(f32[512]{0:T(512)} %param.17) | copy-start | bytes 6148
  51.8 54.5 %all-to-all-start.3 = ((f32[16,96,512]{2,1,0:T(8,128)}), f32[16,96,512]{2,1,0:T(8,128)}, u32[]{:S(2)}, u32[]{:S(2)}) async-start(f32[16,96,512]{2,1,0:T(8,128)} %get-tuple-element.197), calls=%async_computation.3 | async-start | bytes 6291456 | tf_op jit(solution)/shard_map/all_to_all | solution.py:362

commit v2 on v1

v2 whole, which is shorter than its diff:
```python
import jax
import jax.numpy as jnp
from jax import lax
from jax.experimental import pallas as pl
from jax.experimental.pallas import tpu as pltpu
from jax.sharding import PartitionSpec as P

SUB_ROWS = 2
SUB_COLS = 16
STEPS = 4
WASH = 1.5
RECENT = 0.6
EARLIER = 0.3
EXACT = lax.Precision.HIGHEST

OWN = 16
LEV = 5
LIST = 128
SUBS = 2048
HRS = 512
ROWS = 128
COLS = 512
HOPS = LEV
ENT = LEV * LIST

ONE = 64
TWO = 32
DATA = TWO - 1
DEEP = 8
EXTRA = 32
TABLE = 24

F32 = jnp.float32
BF = jnp.bfloat16
I32 = jnp.int32


def nt_dot(a, b):
    return lax.dot_general(a, b, (((1,), (1,)), ((), ())), preferred_element_type=F32)


def nn_dot(a, b):
    return lax.dot_general(a, b, (((1,), (0,)), ((), ())), preferred_element_type=F32)


def iota(shape, dim):
    return lax.broadcasted_iota(I32, shape, dim)


def entry_keys(rows_ref, owner_ref, down_ref, level):
    rows = rows_ref[0, level]
    owner = owner_ref[0, level]
    down = down_ref[0, level]
    valid = (rows >= 0) & (owner >= 0) & (down >= 0)
    return jnp.where(valid, rows, -1), jnp.where(valid, owner * SUBS + down + 1, 0)


def upper_triangle():
    return jnp.where(iota((LIST, LIST), 0) < iota((LIST, LIST), 1), 1.0, 0.0).astype(BF)


def ranks(key_list):
    blocks = []
    for keys in key_list:
        owner = (keys - 1) >> 11
        for level in range(LEV):
            part = owner[:, level * LIST : (level + 1) * LIST]
            blocks.append(jnp.where(iota((OWN, LIST), 0) == part, 1.0, 0.0))
    counts = nn_dot(jnp.concatenate(blocks, axis=0).astype(BF), upper_triangle())
    base = jnp.zeros((OWN, 1), F32)
    pieces = []
    for index, block in enumerate(blocks):
        count = counts[index * OWN : (index + 1) * OWN]
        pieces.append(jnp.sum(block * (count + base), axis=0, keepdims=True))
        base = base + jnp.sum(block, axis=1, keepdims=True)
    out = []
    for index in range(len(key_list)):
        out.append(jnp.concatenate(pieces[index * LEV : (index + 1) * LEV], axis=1).astype(I32))
    return out, base


def all_entries(rows_ref, owner_ref, down_ref):
    both = [entry_keys(rows_ref, owner_ref, down_ref, level) for level in range(LEV)]
    return tuple(jnp.concatenate([pair[k] for pair in both], axis=1) for k in range(2))


def row_columns(table):
    padded = jnp.concatenate([table, jnp.zeros((LIST - OWN, LIST), F32)], axis=0)
    return jnp.transpose(padded).astype(I32) - 1


def pick_rows(column_ref, width, source):
    picks = []
    for owner in range(OWN):
        row = jnp.broadcast_to(column_ref[0:width, owner : owner + 1], (width, 128))
        row = jnp.concatenate([row] * (SUBS // 128), axis=1)
        picks.append(jnp.where(row == iota((width, SUBS), 1), 1.0, 0.0).astype(BF))
    return nn_dot(jnp.concatenate(picks, axis=0), source).reshape(OWN, width, HRS)


def front_kernel(
    rows_ref,
    owner_ref,
    down_ref,
    d_top,
    c_top,
    r_top,
    f_top,
    d_end,
    c_end,
    r_end,
    f_end,
    table_ref,
    rank_ref,
    column_ref,
    last_ref,
    initial_ref,
):
    for index, (top, end) in enumerate(
        ((d_top, d_end), (c_top, c_end), (r_top, r_end), (f_top, f_end))
    ):
        initial_ref[index] = top[0:4, :].astype(F32)
        last_ref[index] = end[4:8, :].astype(F32)
    rows, keys = all_entries(rows_ref, owner_ref, down_ref)
    at_hi = iota((OWN, ENT), 0) == (rows >> 7)
    at_lo = jnp.where(iota((LIST, ENT), 0) == (rows & 127), 1.0, 0.0).astype(BF)
    left = jnp.concatenate(
        [
            jnp.where(at_hi, keys >> 8, 0).astype(F32),
            jnp.where(at_hi, keys & 255, 0).astype(F32),
        ],
        axis=0,
    ).astype(BF)
    both = nt_dot(left, at_lo)
    table = both[:OWN] * 256.0 + both[OWN:]
    (rank,), _ = ranks([keys])
    fits = (keys > 0) & (rank < ONE)
    owner = (keys - 1) >> 11
    goal = ((keys - 1) & (SUBS - 1)) + 1
    at_owner = (iota((OWN, ENT), 0) == owner) & fits
    left = jnp.concatenate(
        [
            jnp.where(at_owner, goal >> 4, 0).astype(F32),
            jnp.where(at_owner, goal & 15, 0).astype(F32),
            jnp.where(at_owner, (rows + 1) >> 4, 0).astype(F32),
            jnp.where(at_owner, (rows + 1) & 15, 0).astype(F32),
        ],
        axis=0,
    ).astype(BF)
    slot = jnp.where(fits, rank, -1)
    at_slot = jnp.where(iota((LIST, ENT), 0) == slot, 1.0, 0.0).astype(BF)
    both = nt_dot(left, at_slot)
    goals = both[:OWN] * 16.0 + both[OWN : 2 * OWN]
    column_ref[...] = row_columns(both[2 * OWN : 3 * OWN] * 16.0 + both[3 * OWN :])
    for owner_id in range(OWN):
        table_ref[owner_id, 0:OWN, :] = table
        table_ref[owner_id, OWN : OWN + 8, :] = jnp.broadcast_to(
            goals[owner_id : owner_id + 1, :], (8, LIST)
        )
    rank_ref[...] = jnp.broadcast_to(rank, (8, ENT))


def gather_kernel(column_ref, hours_ref, send_ref):
    send_ref[...] = pick_rows(column_ref, ONE, hours_ref[0])


def plan_kernel(rows_ref, owner_ref, down_ref, rank_ref, full_ref, column_ref, left_ref, meta_ref):
    full = full_ref[:, 0:OWN, :].reshape(OWN * OWN, LIST).astype(I32)
    parts = jnp.concatenate([(full >> 8).astype(F32), (full & 255).astype(F32)], axis=1)
    parts_t = jnp.transpose(parts).astype(BF)
    rows, first_keys = all_entries(rows_ref, owner_ref, down_ref)
    keys = [first_keys]
    for _ in range(1, HOPS):
        at = keys[-1] - 1
        pick_hi = jnp.where(iota((OWN * OWN, ENT), 0) == (at >> 7), 1.0, 0.0).astype(BF)
        found = nn_dot(parts_t, pick_hi)
        value = found[:LIST] * 256.0 + found[LIST:]
        at_lo = iota((LIST, ENT), 0) == (at & 127)
        keys.append(jnp.sum(jnp.where(at_lo, value, 0.0), axis=0, keepdims=True).astype(I32))
    order = list(range(HOPS - 1, -1, -1))
    first_fits = rank_ref[0:1, :] < ONE
    keys[0] = jnp.where(first_fits, 0, keys[0])
    found, _ = ranks([keys[hop] for hop in order])
    slots = [None] * HOPS
    rest = [None] * HOPS
    for place, hop in enumerate(order):
        limit = DEEP if hop >= 2 else DATA
        used = keys[hop] > 0
        slots[hop] = jnp.where(used & (found[place] < limit), found[place], -1)
        rest[hop] = jnp.where(used & (found[place] >= limit), keys[hop], 0)
    found, totals = ranks([rest[hop] for hop in order])
    most_left = jnp.max(totals, axis=0, keepdims=True)
    for place, hop in enumerate(order):
        left_ref[pl.ds(hop, 1), :] = jnp.where(rest[hop] > 0, found[place], -1)
        left_ref[pl.ds(8 + hop, 1), :] = rest[hop]
    meta = jnp.zeros((5 * OWN, LIST), F32)
    for hop in range(HOPS):
        at = keys[hop] - 1
        owner = at >> 11
        goal = (at & (SUBS - 1)) + 1
        at_owner = (iota((OWN, ENT), 0) == owner) & (slots[hop] >= 0)
        left = jnp.concatenate(
            [
                jnp.where(at_owner, goal >> 4, 0).astype(F32),
                jnp.where(at_owner, goal & 15, 0).astype(F32),
                jnp.where(at_owner, float(hop + 1), 0.0),
                jnp.where(at_owner, (rows + 1) >> 4, 0).astype(F32),
                jnp.where(at_owner, (rows + 1) & 15, 0).astype(F32),
            ],
            axis=0,
        ).astype(BF)
        right = jnp.where(iota((LIST, ENT), 0) == slots[hop], 1.0, 0.0).astype(BF)
        meta = meta + nt_dot(left, right)
    meta_ref[:, 0:128] = meta[:OWN] * 16.0 + meta[OWN : 2 * OWN]
    meta_ref[:, 128:256] = roll(meta[2 * OWN : 3 * OWN], ONE, 1)
    column_ref[...] = row_columns(meta[3 * OWN : 4 * OWN] * 16.0 + meta[4 * OWN :])
    meta_ref[:, 256:384] = jnp.broadcast_to(most_left, (OWN, 128))
    meta_ref[:, 384:512] = jnp.zeros((OWN, 128), F32)


EXT_R = 144
EXT_C = 768


def strip_kernel(d_ref, c_ref, r_ref, f_ref, north_ref, south_ref, west_ref, east_ref):
    lane = iota((ROWS, 128), 1)
    lane4 = iota((4, 128), 1)
    west_ref[...] = jnp.zeros((EXT_R, 128), F32)
    east_ref[...] = jnp.zeros((EXT_R, 128), F32)
    sides = ((west_ref, 0, 0), (east_ref, COLS - 128, 124))
    for out_ref, start, first in sides:
        body = jnp.zeros((ROWS, 128), F32)
        top = jnp.zeros((4, 128), F32)
        bottom = jnp.zeros((4, 128), F32)
        for index, ref in enumerate((d_ref, c_ref, r_ref, f_ref)):
            shift = (4 * index - first) % 128
            block = ref[:, start : start + 128]
            if index == 3:
                block = block.astype(F32)
            mine = (lane >= 4 * index) & (lane < 4 * index + 4)
            mine4 = (lane4 >= 4 * index) & (lane4 < 4 * index + 4)
            body = jnp.where(mine, roll(block, shift, 1), body)
            top = jnp.where(mine4, roll(north_ref[index, :, start : start + 128], shift, 1), top)
            bottom = jnp.where(mine4, roll(south_ref[index, :, start : start + 128], shift, 1), bottom)
        out_ref[8 : 8 + ROWS, :] = body
        out_ref[4:8, :] = top
        out_ref[8 + ROWS : 12 + ROWS, :] = bottom


def shift_lanes(x, places):
    blocks = x.shape[1] // 128
    turned = [roll(x[:, b * 128 : (b + 1) * 128], places, 1) for b in range(blocks)]
    lane = iota(turned[0].shape, 1)
    zero = jnp.zeros_like(turned[0])
    out = []
    for b in range(blocks):
        if places > 0:
            other = turned[b - 1] if b else zero
            out.append(jnp.where(lane < places, other, turned[b]))
        else:
            other = turned[b + 1] if b + 1 < blocks else zero
            out.append(jnp.where(lane >= 128 + places, other, turned[b]))
    return jnp.concatenate(out, axis=1)


def roll(x, shift, axis):
    if shift % x.shape[axis] == 0:
        return x
    return pltpu.roll(x, shift % x.shape[axis], axis)


def main_kernel(
    d_ref,
    c_ref,
    r_ref,
    f_ref,
    north_ref,
    south_ref,
    west_ref,
    east_ref,
    nitro_ref,
    hours_ref,
    rows_ref,
    owner_ref,
    down_ref,
    rank_ref,
    column_ref,
    meta_ref,
    water_out,
    nitro_out,
    excess_out,
    send_ref,
    w_s,
    c_s,
    r_s,
    f_s,
    o_s,
    n_s,
    u_s,
    t_s,
):
    lane = iota((EXT_R, 128), 1)
    for index, (src, dst) in enumerate(((d_ref, w_s), (c_ref, c_s), (r_ref, r_s), (f_ref, f_s))):
        dst[0:8, :] = jnp.zeros((8, EXT_C), F32)
        dst[136:144, :] = jnp.zeros((8, EXT_C), F32)
        body = src[...]
        if index == 3:
            body = body.astype(F32)
        dst[8:136, 128:640] = body
        dst[4:8, 128:640] = north_ref[index]
        dst[136:140, 128:640] = south_ref[index]
        left = roll(west_ref[...], 124 - 4 * index, 1)
        dst[:, 0:128] = jnp.where(lane >= 124, left, 0.0)
        right = roll(east_ref[...], -4 * index, 1)
        dst[:, 640:768] = jnp.where(lane < 4, right, 0.0)
    t_s[...] = jnp.zeros((ROWS, COLS), F32)
    n_s[...] = jnp.zeros((EXT_R + 16, EXT_C), F32)
    u_s[...] = jnp.zeros((EXT_R + 16, EXT_C), F32)
    for _ in range(STEPS):

        def first(chunk, carry):
            at = pl.multiple_of(chunk * 8, 8)
            water = w_s[pl.ds(at, 8), :]
            rate = c_s[pl.ds(at, 8), :] * jnp.exp(jnp.log(water * water) * (1.0 / 3.0))
            out = water * (1.0 - jnp.exp(-rate))
            code = f_s[pl.ds(at, 8), :]
            o_s[pl.ds(at, 8), :] = out
            n_s[pl.ds(at + 8, 8), :] = jnp.where(code == 2.0, out, 0.0)
            u_s[pl.ds(at + 8, 8), :] = jnp.where(code == 3.0, out, 0.0)
            return carry

        lax.fori_loop(0, EXT_R // 8, first, 0, unroll=2)

        for chunk in range(EXT_R // 8):
            at = chunk * 8
            out = o_s[at : at + 8, :]
            code = f_s[at : at + 8, :]
            from_west = shift_lanes(jnp.where(code == 0.0, out, 0.0), 1)
            from_east = shift_lanes(jnp.where(code == 1.0, out, 0.0), -1)
            from_north = n_s[at + 7 : at + 15, :]
            from_south = u_s[at + 9 : at + 17, :]
            total = from_west + from_east + from_north + from_south
            w_s[at : at + 8, :] = w_s[at : at + 8, :] - out + total + r_s[at : at + 8, :]
            if 1 <= chunk <= 16:
                t_s[at - 8 : at, :] = t_s[at - 8 : at, :] + out[:, 128:640]

    nitro_out[...] = nitro_ref[...] * jnp.exp(-WASH * t_s[...])
    water = w_s[8:136, 128:640]
    water_out[...] = water
    blocks = jnp.where(iota((32, COLS), 1) // SUB_COLS == iota((32, COLS), 0), 1.0, 0.0)
    by_row = lax.dot_general(
        blocks, water, (((1,), (1,)), ((), ())), precision=EXACT, preferred_element_type=F32
    )
    pairs = jnp.where(iota((ROWS, 128), 0) // SUB_ROWS == iota((ROWS, 128), 1), 1.0, 0.0)
    means = lax.dot_general(
        by_row, pairs, (((1,), (0,)), ((), ())), precision=EXACT, preferred_element_type=F32
    ) * (1.0 / (SUB_ROWS * SUB_COLS))
    for block in range(ROWS // SUB_ROWS):
        at = block * 32
        factor = jnp.broadcast_to(means[:, block : block + 1], (32, 128))
        factor = jnp.concatenate([factor] * (HRS // 128), axis=1)
        excess = hours_ref[0, at : at + 32, :].astype(F32) * factor
        excess_out[at : at + 32, :] = excess.astype(BF)
    rows, keys = all_entries(rows_ref, owner_ref, down_ref)
    at_block = jnp.where(iota((128, ENT), 0) == (rows >> 5), 1.0, 0.0)
    found = lax.dot_general(
        means, at_block, (((1,), (0,)), ((), ())), precision=EXACT, preferred_element_type=F32
    )
    at_cell = iota((32, ENT), 0) == (rows & 31)
    entry_yield = jnp.sum(jnp.where(at_cell, found, 0.0), axis=0, keepdims=True)
    rank = rank_ref[0:1, :]
    fits = (keys > 0) & (rank < ONE)
    at_owner = (iota((OWN, ENT), 0) == ((keys - 1) >> 11)) & fits
    at_slot = jnp.where(iota((LIST, ENT), 0) == jnp.where(fits, rank, -1), 1.0, 0.0)
    slot_yield = lax.dot_general(
        jnp.where(at_owner, entry_yield, 0.0),
        at_slot,
        (((1,), (1,)), ((), ())),
        precision=EXACT,
        preferred_element_type=F32,
    )
    send_ref[...] = pick_rows(column_ref, TWO, excess_out[...])
    second = meta_ref[:, 128:256] + slot_yield
    for owner in range(OWN):
        send_ref[owner, DATA : DATA + 1, :] = meta_ref[owner : owner + 1, :]
        send_ref[owner, DATA : DATA + 1, 128:256] = second[owner : owner + 1, :]


def lag(x):
    return RECENT * shift_lanes(x, 1) + EARLIER * shift_lanes(x, 2)


TILE = 1024
TILES = SUBS // TILE


def flat_line(lines, width):
    lane = iota((8, 128), 1)
    store = [jnp.zeros((8, 128), F32)] * (OWN * width // 128)
    for src in range(OWN):
        start = src * width
        block, off = start // 128, start % 128
        here = (lane >= off) & (lane < off + width)
        store[block] = jnp.where(here, roll(lines[src], off, 1), store[block])
    return jnp.concatenate(store, axis=1).astype(I32) - 1


def columns_of(lines):
    padded = jnp.concatenate([x[0:1] for x in lines] + [jnp.zeros((128 - OWN, 128), F32)], axis=0)
    return jnp.transpose(padded)


def final_kernel(
    one_ref, two_ref, table_ref, excess_ref, kernel_ref, out_ref, rounds_ref, rows_s, goal_s
):
    step = pl.program_id(0)

    @pl.when(step == 0)
    def _():
        groups = [two_ref[src, TWO - 8 : TWO, :][7:8] for src in range(OWN)]
        goal_s[:, 0 : OWN * ONE] = flat_line([table_ref[src, OWN : OWN + 8, :] for src in range(OWN)], ONE)
        goal_s[:, OWN * ONE :] = flat_line(
            [jnp.broadcast_to(x[:, 0:128], (8, 128)) for x in groups], TWO
        )
        most = groups[0][:, 256:384]
        for x in groups[1:]:
            most = jnp.maximum(most, x[:, 256:384])
        rounds_ref[0, 0] = jnp.max(most).astype(I32)
        factors = columns_of([x[:, 128:256] for x in groups])
        counts = []
        parts = []
        for src in range(OWN):
            factor = jnp.broadcast_to(factors[0 : ONE + TWO, src : src + 1], (ONE + TWO, 128))
            factor = jnp.concatenate([factor] * (HRS // 128), axis=1)
            scaled = one_ref[src] * factor[0:ONE]
            rows_s[src * ONE : (src + 1) * ONE, :] = scaled.astype(BF)
            counts.append(factor[ONE:])
            parts.append(jnp.where(counts[src] > 1.0, lag(two_ref[src]), two_ref[src]))
        deep = jnp.concatenate([x[0:DEEP] for x in parts], axis=0)
        deep_counts = jnp.concatenate([x[0:DEEP] for x in counts], axis=0)
        for hop in range(2, HOPS):
            deep = jnp.where(deep_counts > float(hop), lag(deep), deep)
        for src in range(OWN):
            part = jnp.concatenate([deep[src * DEEP : (src + 1) * DEEP], parts[src][DEEP:]], axis=0)
            high = part.astype(BF)
            at = OWN * ONE + src * TWO
            rows_s[at : at + TWO, :] = high
            at = OWN * (ONE + TWO) + src * TWO
            rows_s[at : at + TWO, :] = (part - high.astype(F32)).astype(BF)

    match = iota((TILE, OWN * (ONE + TWO)), 0) + step * TILE == goal_s[0:1, :]
    put = jnp.where(match, 1.0, 0.0).astype(BF)
    put = jnp.concatenate([put, put[:, OWN * ONE :]], axis=1)
    total = excess_ref[...].astype(F32) + lag(nn_dot(put, rows_s[...]))
    high = total.astype(BF)
    low = (total - high.astype(F32)).astype(BF)
    half = HRS // 2
    parts = jnp.concatenate([high, low], axis=0)
    both = nn_dot(parts[:, :half], kernel_ref[:half, :half])
    out_ref[:, :half] = both[:TILE] + both[TILE:]
    both = nn_dot(parts, kernel_ref[:, half:])
    out_ref[:, half:] = both[:TILE] + both[TILE:]


def neighbours(axis):
    size = lax.axis_size(axis)
    up = [(i, i + 1) for i in range(size - 1)]
    return up, [(j, i) for i, j in up]


def exchange(array):
    return lax.all_to_all(array, "wide", split_axis=0, concat_axis=0, tiled=True)


def exact_dot(left, right):
    return jnp.dot(left, right, precision=EXACT, preferred_element_type=F32)


def routed_local(
    depth_start,
    conveyance,
    cell_rain,
    nitrogen,
    flow_dir,
    unit_hydro,
    rain_hours,
    send_rows,
    send_owner,
    send_down,
):
    lists = (send_rows, send_owner, send_down)
    fields = (depth_start, conveyance, cell_rain, flow_dir)
    whole = lambda shape: pl.BlockSpec(shape, lambda i: (0,) * len(shape))
    table, rank, columns, last, initial = pl.pallas_call(
        front_kernel,
        grid=(1,),
        out_shape=[
            jax.ShapeDtypeStruct((OWN, TABLE, LIST), F32),
            jax.ShapeDtypeStruct((8, ENT), I32),
            jax.ShapeDtypeStruct((LIST, LIST), I32),
            jax.ShapeDtypeStruct((4, 4, COLS), F32),
            jax.ShapeDtypeStruct((4, 4, COLS), F32),
        ],
        in_specs=[whole((1, LEV, 1, LIST))] * 3
        + [pl.BlockSpec((8, COLS), lambda i: (0, 0))] * 4
        + [pl.BlockSpec((8, COLS), lambda i: (ROWS // 8 - 1, 0))] * 4,
        out_specs=[
            whole((OWN, TABLE, LIST)),
            whole((8, ENT)),
            whole((LIST, LIST)),
            whole((4, 4, COLS)),
            whole((4, 4, COLS)),
        ],
        name="front",
    )(*lists, *fields, *fields)
    full = exchange(table)
    up, down = neighbours("wide")
    north = lax.ppermute(last, "wide", up)
    south = lax.ppermute(initial, "wide", down)
    outgoing = pl.pallas_call(
        gather_kernel,
        out_shape=jax.ShapeDtypeStruct((OWN, ONE, HRS), F32),
        grid=(1,),
        in_specs=[whole(x.shape) for x in (columns, rain_hours)],
        out_specs=whole((OWN, ONE, HRS)),
        name="gather_rain",
    )(columns, rain_hours)
    arrived = exchange(outgoing)
    west_strip, east_strip = pl.pallas_call(
        strip_kernel,
        out_shape=[jax.ShapeDtypeStruct((EXT_R, 128), F32)] * 2,
        grid=(1,),
        in_specs=[whole(x.shape) for x in (*fields, north, south)],
        out_specs=[whole((EXT_R, 128))] * 2,
        name="strips",
    )(*fields, north, south)
    up, down = neighbours("narrow")
    west = lax.ppermute(east_strip, "narrow", up)
    east = lax.ppermute(west_strip, "narrow", down)
    columns, left, meta = pl.pallas_call(
        plan_kernel,
        out_shape=[
            jax.ShapeDtypeStruct((LIST, LIST), I32),
            jax.ShapeDtypeStruct((16, ENT), I32),
            jax.ShapeDtypeStruct((OWN, HRS), F32),
        ],
        grid=(1,),
        in_specs=[whole(x.shape) for x in (*lists, rank, full)],
        out_specs=[whole((LIST, LIST)), whole((16, ENT)), whole((OWN, HRS))],
        name="plan",
    )(*lists, rank, full)
    kernel = unit_hydro.astype(BF)
    pattern = jnp.concatenate([kernel, jnp.zeros((HRS,), BF)])
    repeated = jnp.tile(pattern, HRS)[: HRS * (2 * HRS - 1)]
    toeplitz = repeated.reshape(HRS, 2 * HRS - 1)[:, :HRS]
    flow_inputs = (*fields, north, south, west, east, nitrogen, rain_hours)
    flow_inputs += (*lists, rank, columns, meta)
    water, nitrogen_left, excess, outgoing = pl.pallas_call(
        main_kernel,
        out_shape=[
            jax.ShapeDtypeStruct((ROWS, COLS), F32),
            jax.ShapeDtypeStruct((ROWS, COLS), F32),
            jax.ShapeDtypeStruct((SUBS, HRS), BF),
            jax.ShapeDtypeStruct((OWN, TWO, HRS), F32),
        ],
        grid=(1,),
        in_specs=[whole(x.shape) for x in flow_inputs],
        out_specs=[
            whole((ROWS, COLS)),
            whole((ROWS, COLS)),
            whole((SUBS, HRS)),
            whole((OWN, TWO, HRS)),
        ],
        scratch_shapes=[pltpu.VMEM((EXT_R, EXT_C), F32)] * 5
        + [pltpu.VMEM((EXT_R + 16, EXT_C), F32)] * 2
        + [pltpu.VMEM((ROWS, COLS), F32)],
        name="flow_and_send",
    )(*flow_inputs)
    incoming = exchange(outgoing)
    tile = lambda i: (i, 0)
    discharge, most_left = pl.pallas_call(
        final_kernel,
        out_shape=[
            jax.ShapeDtypeStruct((SUBS, HRS), F32),
            jax.ShapeDtypeStruct((1, 1), I32),
        ],
        grid=(TILES,),
        in_specs=[
            whole((OWN, ONE, HRS)),
            whole((OWN, TWO, HRS)),
            whole((OWN, TABLE, LIST)),
            pl.BlockSpec((TILE, HRS), tile),
            whole((HRS, HRS)),
        ],
        out_specs=[
            pl.BlockSpec((TILE, HRS), tile),
            pl.BlockSpec((1, 1), lambda i: (0, 0), memory_space=pltpu.SMEM),
        ],
        scratch_shapes=[
            pltpu.VMEM((OWN * (ONE + 2 * TWO), HRS), BF),
            pltpu.VMEM((8, OWN * (ONE + TWO)), I32),
        ],
        name="route_and_convolve",
    )(arrived, incoming, full, excess, toeplitz)

    def more(state):
        return state[0] * EXTRA < most_left[0, 0]

    def extra_round(state):
        index, flows = state
        valid = (send_rows >= 0) & (send_owner >= 0) & (send_down >= 0)
        rows_column = jnp.where(valid, send_rows, -1).reshape(ENT, 1)
        picker = (rows_column == jnp.arange(SUBS, dtype=I32)[None, :]).astype(F32)
        rows = exact_dot(picker, excess.astype(F32))
        slot_iota = jnp.arange(OWN * EXTRA, dtype=I32)
        send = jnp.zeros((OWN * EXTRA, HRS), F32)
        goals = jnp.zeros((OWN * EXTRA,), F32)
        for hop in range(HOPS):
            key = left[8 + hop] - 1
            rank = left[hop] - index * EXTRA
            here = (left[hop] >= 0) & (rank >= 0) & (rank < EXTRA)
            slot = jnp.where(here, (key >> 11) * EXTRA + rank, -1)
            placer = (slot[None, :] == slot_iota[:, None]).astype(F32)
            send = send + exact_dot(placer, rows)
            goals = goals + jnp.sum(placer * ((key & (SUBS - 1)) + 1).astype(F32)[None, :], axis=1)
            rows = lagged(rows)
        came = exchange(send.reshape(OWN, EXTRA, HRS)).reshape(-1, HRS)
        came_goals = exchange(goals.reshape(OWN, EXTRA)).reshape(-1).astype(I32) - 1
        routed = exact_dot(lagged(came), toeplitz.astype(F32))
        receiver = (came_goals[None, :] == jnp.arange(SUBS, dtype=I32)[:, None]).astype(F32)
        return index + 1, flows + exact_dot(receiver, routed)

    discharge = lax.while_loop(more, extra_round, (jnp.zeros((), I32), discharge))[1]
    return (water, nitrogen_left, discharge[None])


def lagged(flows):
    one_back = jnp.pad(flows, ((0, 0), (1, 0)))[:, :-1]
    two_back = jnp.pad(flows, ((0, 0), (2, 0)))[:, :-2]
    return RECENT * one_back + EARLIER * two_back


def solution(mesh):
    placed = (
        P("wide", "narrow"),
        P("wide", "narrow"),
        P("wide", "narrow"),
        P("wide", "narrow"),
        P("wide", "narrow"),
        P(),
        P("narrow", "wide", None),
        P("narrow", None, "wide", None),
        P("narrow", None, "wide", None),
        P("narrow", None, "wide", None),
    )
    return jax.shard_map(
        routed_local,
        mesh=mesh,
        in_specs=placed,
        out_specs=(P("wide", "narrow"), P("wide", "narrow"), P("narrow", "wide", None)),
        check_vma=False,
    )
```

time: 129 us -> 122 us (0.946)
  waiting for transfers between devices: 54.3 us -> 43 us
  starting transfers between devices: 21.8 us -> 28.5 us
  local copies, waits for them, and re-layouts: 6.55 us -> 9.47 us
  Pallas kernels: 37.6 us -> 34.9 us
  other arithmetic: 2.25 us -> 0.06 us
    all_to_all x2 -> x3, waiting for transfers between devices: 51.4 us -> 38.3 us  [exchange(): lax.all_to_all(array, 'wide', split_axis=0, concat_axis=0, tiled=True)]
    all_to_all x2 -> x3, starting transfers between devices: 14.4 us -> 20.8 us  [exchange(): lax.all_to_all(array, 'wide', split_axis=0, concat_axis=0, tiled=True)]
    unnamed x20 -> x24, local copies, waits for them, and re-layouts: 2.44 us -> 5.71 us
    pallas_call x5 -> x6, Pallas kernels: 37.6 us -> 34.9 us  [the longest x1 12.4 us: routed_local(): pl.pallas_call(final_kernel, out_shape=[jax.ShapeDtypeStruct((SUBS, HRS),...]
    ppermute x4, waiting for transfers between devices: 2.9 us -> 4.72 us  [the longest x1 4.12 us: routed_local(): south = lax.ppermute(initial, 'wide', down)]
    another operation x2 -> x0, local copies, waits for them, and re-layouts: 1.53 us -> none  [local(): initial = jnp.stack([x[:4].astype(F32) for x in fields])]
    reduce_max x1 -> x0, other arithmetic: 1.46 us -> none  [local(): most_left = jnp.max(incoming[:, DATA, 256])]
    reshape x2 -> x1, local copies, waits for them, and re-layouts: 2.55 us -> 2.91 us  [routed_local(): toeplitz = repeated.reshape(HRS, 2 * HRS - 1)[:, :HRS]]
  transfers between devices with their start and end apart: 6 -> 7, of which waited for: 3 -> 4; matrix products, arithmetic and copies ran while one was open for 5% -> 7% of each run, Pallas kernels for 4% -> 9%
where the time goes in v2:
time: 122 us; the launch traced here: 121 us
  waiting for transfers between devices  43 us (35%)
  Pallas kernels  34.9 us (29%)
  starting transfers between devices  28.5 us (23%)
  local copies, waits for them, and re-layouts  9.47 us (8%)
  matrix products  3.15 us (3%)
    all_to_all x3, waiting for transfers between devices, exchange(): lax.all_to_all(array, 'wide', split_axis=0, concat_axis=0, tiled=True)  38.3 us
    all_to_all x3, starting transfers between devices, exchange(): lax.all_to_all(array, 'wide', split_axis=0, concat_axis=0, tiled=True)  20.8 us
    pallas_call x1, Pallas kernels, routed_local(): pl.pallas_call(final_kernel, out_shape=[jax.ShapeDtypeStruct((SUBS, HRS),...  12.4 us
    pallas_call x1, Pallas kernels, routed_local(): pl.pallas_call(main_kernel, out_shape=[jax.ShapeDtypeStruct((ROWS, COLS),...  9.41 us
    unnamed x24, local copies, waits for them, and re-layouts  5.71 us
    pallas_call x1, Pallas kernels, routed_local(): pl.pallas_call(gather_kernel, out_shape=jax.ShapeDtypeStruct((OWN, ONE, H...  5.33 us
    ppermute x1, waiting for transfers between devices, routed_local(): south = lax.ppermute(initial, 'wide', down)  4.12 us
    ppermute x1, starting transfers between devices, routed_local(): north = lax.ppermute(last, 'wide', up)  3.82 us
  transfers between devices with their start and end apart: 7, of which 4 were waited for; matrix products, arithmetic and copies ran while one was open for 7% of the time, Pallas kernels for 9%

profile of v2, /device:TPU:0, one launch (start us, length us, event | category | flops | bytes accessed | tf_op | source)
XLA Modules:
  0.0 120.7 jit_solution(12870567602100704105)
XLA Ops:
  0.6 2.0 %front.1 = (f32[16,24,128]{2,1,0:T(8,128)}, s32[8,640]{1,0:T(8,128)}, s32[128,128]{1,0:T(8,128)}, f32[4,4,512]{2,1,0:T(4,128)}, f32[4,4,512]{2,1,0:T(4,128)}) custom-call(s32[1,5,1,128]{3,2,1,0:T(1,128)} %rows_ref.5, s32[1,5,1,128]{3,2,1,0:T(1,128)} %owner_ref.5, s32[1,5,1,128]{3,2,1,0:T(1,128)} %down_ref.5, f32[128,512]{1,0:T(8,128)} %d_ref.3, ...), custom_call_target="tpu_custom_call" | custom-call | tf_op jit(solution)/shard_map/front/pallas_call | solution.py:494
  2.7 8.0 %all-to-all-start.2 = ((f32[16,24,128]{2,1,0:T(8,128)}), f32[16,24,128]{2,1,0:T(8,128)S(1)}, u32[]{:S(2)}, u32[]{:S(2)}) async-start(f32[16,24,128]{2,1,0:T(8,128)} %get-tuple-element.233), calls=%async_computation.2 | async-start | bytes 393216 | tf_op jit(solution)/shard_map/all_to_all | solution.py:472
  10.7 3.8 %collective-permute-start = (f32[4,4,512]{2,1,0:T(4,128)}, f32[4,4,512]{2,1,0:T(4,128)S(1)}, u32[]{:S(2)}, u32[]{:S(2)}) collective-permute-start(f32[4,4,512]{2,1,0:T(4,128)} %get-tuple-element.228), channel_id=1, source_target_pairs={{0,8},{8,16},{16,24},{24,32},{32,40},{40,48},{48,56},{56,64},{64,7... | collective-permute-start | bytes 98312 | tf_op jit(solution)/shard_map/ppermute | solution.py:518
  14.5 1.3 %collective-permute-start.1 = (f32[4,4,512]{2,1,0:T(4,128)}, f32[4,4,512]{2,1,0:T(4,128)S(1)}, u32[]{:S(2)}, u32[]{:S(2)}) collective-permute-start(f32[4,4,512]{2,1,0:T(4,128)} %get-tuple-element.229), channel_id=1, source_target_pairs={{8,0},{16,8},{24,16},{32,24},{40,32},{48,40},{56,48},{64,56},{72,6... | collective-permute-start | bytes 98312 | tf_op jit(solution)/shard_map/ppermute | solution.py:519
  15.8 0.6 collective-permute-done.north_ref
  16.4 4.1 %collective-permute-done.1.south_ref = f32[4,4,512]{2,1,0:T(4,128)S(1)} collective-permute-done((f32[4,4,512]{2,1,0:T(4,128)}, f32[4,4,512]{2,1,0:T(4,128)S(1)}, u32[]{:S(2)}, u32[]{:S(2)}) %collective-permute-start.1) | collective-permute-done | bytes 32800 | tf_op jit(solution)/shard_map/ppermute | solution.py:519
  20.5 0.6 copy-done.5
  21.1 2.0 %strips.1 = (f32[144,128]{1,0:T(8,128)}, f32[144,128]{1,0:T(8,128)}) custom-call(f32[128,512]{1,0:T(8,128)} %d_ref.3, f32[128,512]{1,0:T(8,128)} %c_ref.3, f32[128,512]{1,0:T(8,128)} %r_ref.3, s32[128,512]{1,0:T(8,128)} %f_ref.3, f32[4,4,512]{2,1,0:T(4,128)} %copy-done.4, f32[4,4,512]{2,1,0:T(4,128)} %copy-done.5), custom_call_target="tpu_custom_call" | custom-call | tf_op jit(solution)/shard_map/strips/pallas_call | solution.py:529
  23.1 1.3 %collective-permute-start.2 = (f32[144,128]{1,0:T(8,128)}, f32[144,128]{1,0:T(8,128)S(1)}, u32[]{:S(2)}, u32[]{:S(2)}) collective-permute-start(f32[144,128]{1,0:T(8,128)} %get-tuple-element.230), channel_id=1, source_target_pairs={{0,1},{1,2},{2,3},{3,4},{4,5},{5,6},{6,7},{8,9},{9,10},{10,11},{11... | collective-permute-start | bytes 221192 | tf_op jit(solution)/shard_map/ppermute | solution.py:538
  24.4 1.3 %collective-permute-start.3 = (f32[144,128]{1,0:T(8,128)}, f32[144,128]{1,0:T(8,128)S(1)}, u32[]{:S(2)}, u32[]{:S(2)}) collective-permute-start(f32[144,128]{1,0:T(8,128)} %get-tuple-element.231), channel_id=1, source_target_pairs={{1,0},{2,1},{3,2},{4,3},{5,4},{6,5},{7,6},{9,8},{10,9},{11,10},{12... | collective-permute-start | bytes 221192 | tf_op jit(solution)/shard_map/ppermute | solution.py:539
  25.7 0.0 all-to-all-done.2.full_ref.table_ref
  25.8 0.7 copy-done.3
  26.4 3.7 %plan.1 = (s32[128,128]{1,0:T(8,128)}, s32[16,640]{1,0:T(8,128)S(1)}, f32[16,512]{1,0:T(8,128)}) custom-call(s32[1,5,1,128]{3,2,1,0:T(1,128)} %rows_ref.5, s32[1,5,1,128]{3,2,1,0:T(1,128)} %owner_ref.5, s32[1,5,1,128]{3,2,1,0:T(1,128)} %down_ref.5, s32[8,640]{1,0:T(8,128)} %get-tuple-element.232.rank_ref, f32[16,24,128]{2,1,0:T(8,128)} %copy-done.3), custom_call_target="tpu_custom_call" | custom-call | tf_op jit(solution)/shard_map/plan/pallas_call | solution.py:540
  30.1 0.0 collective-permute-done.2.west_ref
  30.1 0.0 collective-permute-done.3.east_ref
  30.1 0.6 copy-done.6
  30.7 0.0 copy-done.7
  30.8 9.4 %flow_and_send.1 = (f32[128,512]{1,0:T(8,128)}, f32[128,512]{1,0:T(8,128)}, bf16[2048,512]{1,0:T(8,128)(2,1)}, f32[16,32,512]{2,1,0:T(8,128)}) custom-call(f32[128,512]{1,0:T(8,128)} %d_ref.3, f32[128,512]{1,0:T(8,128)} %c_ref.3, f32[128,512]{1,0:T(8,128)} %r_ref.3, s32[128,512]{1,0:T(8,128)} %f_ref.3, f32[4,4,512]{2,1,0:T(4,128)} %copy-done.4, ...), custom_call_target="tpu_custom_call" | custom-call | tf_op jit(solution)/shard_map/flow_and_send/pallas_call | solution.py:558
  40.2 8.3 %all-to-all-start.4 = ((f32[16,32,512]{2,1,0:T(8,128)}), f32[16,32,512]{2,1,0:T(8,128)S(1)}, u32[]{:S(2)}, u32[]{:S(2)}) async-start(f32[16,32,512]{2,1,0:T(8,128)} %get-tuple-element.239), calls=%async_computation.4 | async-start | bytes 2097152 | tf_op jit(solution)/shard_map/all_to_all | solution.py:472
  48.5 5.3 %gather_rain.1 = f32[16,64,512]{2,1,0:T(8,128)} custom-call(s32[128,128]{1,0:T(8,128)} %get-tuple-element.238.column_ref, bf16[1,2048,512]{2,1,0:T(8,128)(2,1)} %hours_ref.3), custom_call_target="tpu_custom_call" | custom-call | tf_op jit(solution)/shard_map/gather_rain/pallas_call | solution.py:520
  53.8 11.6 %all-to-all-done.4.two_ref = f32[16,32,512]{2,1,0:T(8,128)S(1)} async-done(((f32[16,32,512]{2,1,0:T(8,128)}), f32[16,32,512]{2,1,0:T(8,128)S(1)}, u32[]{:S(2)}, u32[]{:S(2)}) %all-to-all-start.4) | async-done | bytes 1048608 | tf_op jit(solution)/shard_map/all_to_all | solution.py:472
  65.4 1.0 copy-done.1
  66.4 4.5 %all-to-all-start.3 = ((f32[16,64,512]{2,1,0:T(8,128)}), f32[16,64,512]{2,1,0:T(8,128)S(1)}, u32[]{:S(2)}, u32[]{:S(2)}) async-start(f32[16,64,512]{2,1,0:T(8,128)} %gather_rain.1), calls=%async_computation.3 | async-start | bytes 4194304 | tf_op jit(solution)/shard_map/all_to_all | solution.py:472
  70.9 0.2 broadcast_bitcast_fusion
  71.2 1.3 %copy.13 = bf16[64,8,8,128]{3,1,2,0:T(8,128)(2,1)} copy(bf16[64,8,8,128]{3,2,1,0:T(8,128)(2,1)S(1)} %broadcast_bitcast_fusion) | data formatting | bytes 2097152
  72.5 2.9 %reshape.173 = bf16[512,1023]{1,0:T(8,128)(2,1)S(1)} reshape(bf16[523776]{0:T(1024)(128)(2,1)} %bitcast.47) | data formatting | bytes 2095104 | tf_op jit(solution)/shard_map/reshape | solution.py:555
  75.4 0.8 slice.174.kernel_ref
  76.3 3.1 %fusion.44 = f32[640,512]{1,0:T(8,128)S(1)} fusion(bf16[2048,512]{1,0:T(8,128)(2,1)} %get-tuple-element.240.excess_ref, s32[640]{0:T(1024)S(1)} %bitcast_select_fusion), kind=kOutput, calls=%fused_computation.83 | convolution fusion | flops 1343488000 | bytes 3410432 | tf_op jit(solution)/shard_map/while/body/dot_general | solution.py:476
  79.4 26.7 %all-to-all-done.3.one_ref = f32[16,64,512]{2,1,0:T(8,128)S(1)} async-done(((f32[16,64,512]{2,1,0:T(8,128)}), f32[16,64,512]{2,1,0:T(8,128)S(1)}, u32[]{:S(2)}, u32[]{:S(2)}) %all-to-all-start.3) | async-done | bytes 2097184 | tf_op jit(solution)/shard_map/all_to_all | solution.py:472
  106.1 1.3 %copy-done = f32[16,64,512]{2,1,0:T(8,128)} copy-done((f32[16,64,512]{2,1,0:T(8,128)}, f32[16,64,512]{2,1,0:T(8,128)S(1)}, u32[]{:S(2)}) %copy-start) | copy-done | bytes 2097176
  107.4 12.4 %route_and_convolve.1 = (f32[2048,512]{1,0:T(8,128)}, s32[1,1]{1,0:T(1,128)}) custom-call(f32[16,64,512]{2,1,0:T(8,128)} %copy-done, f32[16,32,512]{2,1,0:T(8,128)} %copy-done.1, f32[16,24,128]{2,1,0:T(8,128)} %copy-done.3, bf16[2048,512]{1,0:T(8,128)(2,1)} %get-tuple-element.240.excess_ref, bf16[512,512]{1,0:T(8,128)(2,1)} %slice.174.kernel_ref), custom_call_target="tpu_custom_call" | custom-call | tf_op jit(solution)/shard_map/route_and_convolve/pallas_call | solution.py:581
  119.8 0.7 while.14
  (21 shorter events, 0.1 us)
Async XLA Ops:
  2.7 23.1 %all-to-all-start.2 = ((f32[16,24,128]{2,1,0:T(8,128)}), f32[16,24,128]{2,1,0:T(8,128)S(1)}, u32[]{:S(2)}, u32[]{:S(2)}) async-start(f32[16,24,128]{2,1,0:T(8,128)} %get-tuple-element.233), calls=%async_computation.2 | async-start | bytes 393216 | tf_op jit(solution)/shard_map/all_to_all | solution.py:472
  10.7 5.7 %collective-permute-start = (f32[4,4,512]{2,1,0:T(4,128)}, f32[4,4,512]{2,1,0:T(4,128)S(1)}, u32[]{:S(2)}, u32[]{:S(2)}) collective-permute-start(f32[4,4,512]{2,1,0:T(4,128)} %get-tuple-element.228), channel_id=1, source_target_pairs={{0,8},{8,16},{16,24},{24,32},{32,40},{40,48},{48,56},{56,64},{64,7... | collective-permute-start | bytes 98312 | tf_op jit(solution)/shard_map/ppermute | solution.py:518
  14.5 6.0 %collective-permute-start.1 = (f32[4,4,512]{2,1,0:T(4,128)}, f32[4,4,512]{2,1,0:T(4,128)S(1)}, u32[]{:S(2)}, u32[]{:S(2)}) collective-permute-start(f32[4,4,512]{2,1,0:T(4,128)} %get-tuple-element.229), channel_id=1, source_target_pairs={{8,0},{16,8},{24,16},{32,24},{40,32},{48,40},{56,48},{64,56},{72,6... | collective-permute-start | bytes 98312 | tf_op jit(solution)/shard_map/ppermute | solution.py:519
  16.4 4.1 %copy-start.4 = (f32[4,4,512]{2,1,0:T(4,128)}, f32[4,4,512]{2,1,0:T(4,128)S(1)}, u32[]{:S(2)}) copy-start(f32[4,4,512]{2,1,0:T(4,128)S(1)} %collective-permute-done.north_ref) | copy-start | bytes 98308
  20.5 0.6 copy-start.5
  23.1 7.0 %collective-permute-start.2 = (f32[144,128]{1,0:T(8,128)}, f32[144,128]{1,0:T(8,128)S(1)}, u32[]{:S(2)}, u32[]{:S(2)}) collective-permute-start(f32[144,128]{1,0:T(8,128)} %get-tuple-element.230), channel_id=1, source_target_pairs={{0,1},{1,2},{2,3},{3,4},{4,5},{5,6},{6,7},{8,9},{9,10},{10,11},{11... | collective-permute-start | bytes 221192 | tf_op jit(solution)/shard_map/ppermute | solution.py:538
  24.4 5.7 %collective-permute-start.3 = (f32[144,128]{1,0:T(8,128)}, f32[144,128]{1,0:T(8,128)S(1)}, u32[]{:S(2)}, u32[]{:S(2)}) collective-permute-start(f32[144,128]{1,0:T(8,128)} %get-tuple-element.231), channel_id=1, source_target_pairs={{1,0},{2,1},{3,2},{4,3},{5,4},{6,5},{7,6},{9,8},{10,9},{11,10},{12... | collective-permute-start | bytes 221192 | tf_op jit(solution)/shard_map/ppermute | solution.py:539
  25.7 0.7 copy-start.3
  30.1 0.6 copy-start.6
  30.1 0.6 copy-start.7
  40.2 25.2 %all-to-all-start.4 = ((f32[16,32,512]{2,1,0:T(8,128)}), f32[16,32,512]{2,1,0:T(8,128)S(1)}, u32[]{:S(2)}, u32[]{:S(2)}) async-start(f32[16,32,512]{2,1,0:T(8,128)} %get-tuple-element.239), calls=%async_computation.4 | async-start | bytes 2097152 | tf_op jit(solution)/shard_map/all_to_all | solution.py:472
  53.8 17.1 %copy-start.11 = (f32[512]{0:T(512)S(1)}, f32[512]{0:T(512)}, u32[]{:S(2)}) copy-start(f32[512]{0:T(512)} %param.17) | copy-start | bytes 6148
  53.8 17.1 %copy-start.8 = (s32[1,5,1,128]{3,2,1,0:T(1,128)S(1)}, s32[1,5,1,128]{3,2,1,0:T(1,128)}, u32[]{:S(2)}) copy-start(s32[1,5,1,128]{3,2,1,0:T(1,128)} %rows_ref.5) | copy-start | bytes 7684
  65.4 1.0 copy-start.1
  66.4 39.7 %all-to-all-start.3 = ((f32[16,64,512]{2,1,0:T(8,128)}), f32[16,64,512]{2,1,0:T(8,128)S(1)}, u32[]{:S(2)}, u32[]{:S(2)}) async-start(f32[16,64,512]{2,1,0:T(8,128)} %gather_rain.1), calls=%async_computation.3 | async-start | bytes 4194304 | tf_op jit(solution)/shard_map/all_to_all | solution.py:472
  72.5 3.8 %copy-start.9 = (s32[1,5,1,128]{3,2,1,0:T(1,128)S(1)}, s32[1,5,1,128]{3,2,1,0:T(1,128)}, u32[]{:S(2)}) copy-start(s32[1,5,1,128]{3,2,1,0:T(1,128)} %owner_ref.5) | copy-start | bytes 7684
  72.5 3.8 %copy-start.10 = (s32[1,5,1,128]{3,2,1,0:T(1,128)S(1)}, s32[1,5,1,128]{3,2,1,0:T(1,128)}, u32[]{:S(2)}) copy-start(s32[1,5,1,128]{3,2,1,0:T(1,128)} %down_ref.5) | copy-start | bytes 7684
  106.1 1.3 %copy-start = (f32[16,64,512]{2,1,0:T(8,128)}, f32[16,64,512]{2,1,0:T(8,128)S(1)}, u32[]{:S(2)}) copy-start(f32[16,64,512]{2,1,0:T(8,128)S(1)} %all-to-all-done.3.one_ref) | copy-start | bytes 6291460

commit v3 on v2

--- a/solution.py
+++ b/solution.py
@@ -33,6 +33,8 @@
 F32 = jnp.float32
 BF = jnp.bfloat16
 I32 = jnp.int32
+
+ROOM = pltpu.CompilerParams(vmem_limit_bytes=26 << 20)
 
 
 def nt_dot(a, b):
@@ -112,7 +114,6 @@
     f_end,
     table_ref,
     rank_ref,
-    column_ref,
     last_ref,
     initial_ref,
 ):
@@ -142,16 +143,13 @@
         [
             jnp.where(at_owner, goal >> 4, 0).astype(F32),
             jnp.where(at_owner, goal & 15, 0).astype(F32),
-            jnp.where(at_owner, (rows + 1) >> 4, 0).astype(F32),
-            jnp.where(at_owner, (rows + 1) & 15, 0).astype(F32),
         ],
         axis=0,
     ).astype(BF)
     slot = jnp.where(fits, rank, -1)
     at_slot = jnp.where(iota((LIST, ENT), 0) == slot, 1.0, 0.0).astype(BF)
     both = nt_dot(left, at_slot)
-    goals = both[:OWN] * 16.0 + both[OWN : 2 * OWN]
-    column_ref[...] = row_columns(both[2 * OWN : 3 * OWN] * 16.0 + both[3 * OWN :])
+    goals = both[:OWN] * 16.0 + both[OWN:]
     for owner_id in range(OWN):
         table_ref[owner_id, 0:OWN, :] = table
         table_ref[owner_id, OWN : OWN + 8, :] = jnp.broadcast_to(
@@ -160,12 +158,42 @@
     rank_ref[...] = jnp.broadcast_to(rank, (8, ENT))
 
 
-def gather_kernel(column_ref, hours_ref, send_ref):
-    send_ref[...] = pick_rows(column_ref, ONE, hours_ref[0])
-
-
-def plan_kernel(rows_ref, owner_ref, down_ref, rank_ref, full_ref, column_ref, left_ref, meta_ref):
-    full = full_ref[:, 0:OWN, :].reshape(OWN * OWN, LIST).astype(I32)
+def gather_kernel(rows_ref, owner_ref, down_ref, hours_ref, send_ref, column_s):
+    rows, keys = all_entries(rows_ref, owner_ref, down_ref)
+    (rank,), _ = ranks([keys])
+    fits = (keys > 0) & (rank < ONE)
+    at_owner = (iota((OWN, ENT), 0) == ((keys - 1) >> 11)) & fits
+    left = jnp.concatenate(
+        [
+            jnp.where(at_owner, (rows + 1) >> 4, 0).astype(F32),
+            jnp.where(at_owner, (rows + 1) & 15, 0).astype(F32),
+        ],
+        axis=0,
+    ).astype(BF)
+    slot = jnp.where(fits, rank, -1)
+    at_slot = jnp.where(iota((LIST, ENT), 0) == slot, 1.0, 0.0).astype(BF)
+    both = nt_dot(left, at_slot)
+    column_s[...] = row_columns(both[:OWN] * 16.0 + both[OWN:])
+    send_ref[...] = pick_rows(column_s, ONE, hours_ref[0])
+
+
+def plan_kernel(
+    rows_ref,
+    owner_ref,
+    down_ref,
+    rank_ref,
+    full_ref,
+    column_ref,
+    hop_ref,
+    goal_ref,
+    left_ref,
+    meta_ref,
+    full_s,
+):
+    pltpu.sync_copy(full_ref, full_s)
+    for owner in range(OWN):
+        goal_ref[owner : owner + 1, :] = full_s[owner, OWN : OWN + 8, :][0:1]
+    full = full_s[:, 0:OWN, :].reshape(OWN * OWN, LIST).astype(I32)
     parts = jnp.concatenate([(full >> 8).astype(F32), (full & 255).astype(F32)], axis=1)
     parts_t = jnp.transpose(parts).astype(BF)
     rows, first_keys = all_entries(rows_ref, owner_ref, down_ref)
@@ -180,7 +208,7 @@
     order = list(range(HOPS - 1, -1, -1))
     first_fits = rank_ref[0:1, :] < ONE
     keys[0] = jnp.where(first_fits, 0, keys[0])
-    found, _ = ranks([keys[hop] for hop in order])
+    found, listed = ranks([keys[hop] for hop in order])
     slots = [None] * HOPS
     rest = [None] * HOPS
     for place, hop in enumerate(order):
@@ -211,8 +239,11 @@
         ).astype(BF)
         right = jnp.where(iota((LIST, ENT), 0) == slots[hop], 1.0, 0.0).astype(BF)
         meta = meta + nt_dot(left, right)
-    meta_ref[:, 0:128] = meta[:OWN] * 16.0 + meta[OWN : 2 * OWN]
-    meta_ref[:, 128:256] = roll(meta[2 * OWN : 3 * OWN], ONE, 1)
+    goals = meta[:OWN] * 16.0 + meta[OWN : 2 * OWN]
+    scan = jnp.minimum(listed, float(DATA)) + 1.0
+    meta_ref[:, 0:128] = jnp.where(iota((OWN, LIST), 1) == LIST - 1, scan, goals)
+    meta_ref[:, 128:256] = jnp.zeros((OWN, 128), F32)
+    hop_ref[...] = row_columns(meta[2 * OWN : 3 * OWN] + 1.0)
     column_ref[...] = row_columns(meta[3 * OWN : 4 * OWN] * 16.0 + meta[4 * OWN :])
     meta_ref[:, 256:384] = jnp.broadcast_to(most_left, (OWN, 128))
     meta_ref[:, 384:512] = jnp.zeros((OWN, 128), F32)
@@ -222,7 +253,20 @@
 EXT_C = 768
 
 
-def strip_kernel(d_ref, c_ref, r_ref, f_ref, north_ref, south_ref, west_ref, east_ref):
+def fetch(sources, places, sems):
+    copies = [
+        pltpu.make_async_copy(src, dst, sems.at[k]) for k, (src, dst) in enumerate(zip(sources, places))
+    ]
+    for copy in copies:
+        copy.start()
+    for copy in copies:
+        copy.wait()
+
+
+def strip_kernel(
+    d_ref, c_ref, r_ref, f_ref, north_any, south_any, west_ref, east_ref, north_ref, south_ref, sems
+):
+    fetch((north_any, south_any), (north_ref, south_ref), sems)
     lane = iota((ROWS, 128), 1)
     lane4 = iota((4, 128), 1)
     west_ref[...] = jnp.zeros((EXT_R, 128), F32)
@@ -274,10 +318,10 @@
     c_ref,
     r_ref,
     f_ref,
-    north_ref,
-    south_ref,
-    west_ref,
-    east_ref,
+    north_any,
+    south_any,
+    west_any,
+    east_any,
     nitro_ref,
     hours_ref,
     rows_ref,
@@ -285,6 +329,7 @@
     down_ref,
     rank_ref,
     column_ref,
+    hop_ref,
     meta_ref,
     water_out,
     nitro_out,
@@ -298,7 +343,14 @@
     n_s,
     u_s,
     t_s,
+    north_ref,
+    south_ref,
+    west_ref,
+    east_ref,
+    sems,
 ):
+    edges = (north_any, south_any, west_any, east_any)
+    fetch(edges, (north_ref, south_ref, west_ref, east_ref), sems)
     lane = iota((EXT_R, 128), 1)
     for index, (src, dst) in enumerate(((d_ref, w_s), (c_ref, c_s), (r_ref, r_s), (f_ref, f_s))):
         dst[0:8, :] = jnp.zeros((8, EXT_C), F32)
@@ -379,11 +431,22 @@
         precision=EXACT,
         preferred_element_type=F32,
     )
-    send_ref[...] = pick_rows(column_ref, TWO, excess_out[...])
-    second = meta_ref[:, 128:256] + slot_yield
+    picked = pick_rows(column_ref, TWO, excess_out[...])
+    counts = []
+    parts = []
     for owner in range(OWN):
+        count = jnp.broadcast_to(hop_ref[0:TWO, owner : owner + 1], (TWO, 128))
+        counts.append(jnp.concatenate([count] * (HRS // 128), axis=1))
+        parts.append(jnp.where(counts[owner] > 1, lag(picked[owner]), picked[owner]))
+    deep = jnp.concatenate([x[0:DEEP] for x in parts], axis=0)
+    deep_counts = jnp.concatenate([x[0:DEEP] for x in counts], axis=0)
+    for hop in range(2, HOPS):
+        deep = jnp.where(deep_counts > hop, lag(deep), deep)
+    for owner in range(OWN):
+        send_ref[owner, 0:DEEP, :] = deep[owner * DEEP : (owner + 1) * DEEP]
+        send_ref[owner, DEEP:, :] = parts[owner][DEEP:]
         send_ref[owner, DATA : DATA + 1, :] = meta_ref[owner : owner + 1, :]
-        send_ref[owner, DATA : DATA + 1, 128:256] = second[owner : owner + 1, :]
+        send_ref[owner, DATA : DATA + 1, 128:256] = slot_yield[owner : owner + 1, :]
 
 
 def lag(x):
@@ -411,47 +474,55 @@
 
 
 def final_kernel(
-    one_ref, two_ref, table_ref, excess_ref, kernel_ref, out_ref, rounds_ref, rows_s, goal_s
+    one_ref,
+    two_ref,
+    goal_ref,
+    excess_ref,
+    kernel_ref,
+    out_ref,
+    rounds_ref,
+    rows_s,
+    line_s,
+    goal_s,
+    sum_s,
+    target_s,
 ):
     step = pl.program_id(0)
 
     @pl.when(step == 0)
     def _():
         groups = [two_ref[src, TWO - 8 : TWO, :][7:8] for src in range(OWN)]
-        goal_s[:, 0 : OWN * ONE] = flat_line([table_ref[src, OWN : OWN + 8, :] for src in range(OWN)], ONE)
-        goal_s[:, OWN * ONE :] = flat_line(
-            [jnp.broadcast_to(x[:, 0:128], (8, 128)) for x in groups], TWO
+        for src in range(OWN):
+            line_s[src : src + 1, :] = groups[src][:, 0:128].astype(I32) - 1
+        pltpu.sync_copy(line_s, target_s)
+        sum_s[...] = jnp.zeros(sum_s.shape, F32)
+        for src in range(OWN):
+
+            def add_row(slot, carry):
+                target = target_s[src, slot]
+                target = jnp.where(target >= 0, target, SUBS)
+                row = two_ref[src, pl.ds(slot, 1), :]
+                sum_s[pl.ds(target, 1), :] = sum_s[pl.ds(target, 1), :] + row
+                return carry
+
+            lax.fori_loop(0, target_s[src, LIST - 1], add_row, 0)
+        goal_s[...] = flat_line(
+            [jnp.broadcast_to(goal_ref[src : src + 1, :], (8, 128)) for src in range(OWN)], ONE
         )
         most = groups[0][:, 256:384]
         for x in groups[1:]:
             most = jnp.maximum(most, x[:, 256:384])
         rounds_ref[0, 0] = jnp.max(most).astype(I32)
         factors = columns_of([x[:, 128:256] for x in groups])
-        counts = []
-        parts = []
         for src in range(OWN):
-            factor = jnp.broadcast_to(factors[0 : ONE + TWO, src : src + 1], (ONE + TWO, 128))
+            factor = jnp.broadcast_to(factors[0:ONE, src : src + 1], (ONE, 128))
             factor = jnp.concatenate([factor] * (HRS // 128), axis=1)
-            scaled = one_ref[src] * factor[0:ONE]
-            rows_s[src * ONE : (src + 1) * ONE, :] = scaled.astype(BF)
-            counts.append(factor[ONE:])
-            parts.append(jnp.where(counts[src] > 1.0, lag(two_ref[src]), two_ref[src]))
-        deep = jnp.concatenate([x[0:DEEP] for x in parts], axis=0)
-        deep_counts = jnp.concatenate([x[0:DEEP] for x in counts], axis=0)
-        for hop in range(2, HOPS):
-            deep = jnp.where(deep_counts > float(hop), lag(deep), deep)
-        for src in range(OWN):
-            part = jnp.concatenate([deep[src * DEEP : (src + 1) * DEEP], parts[src][DEEP:]], axis=0)
-            high = part.astype(BF)
-            at = OWN * ONE + src * TWO
-            rows_s[at : at + TWO, :] = high
-            at = OWN * (ONE + TWO) + src * TWO
-            rows_s[at : at + TWO, :] = (part - high.astype(F32)).astype(BF)
-
-    match = iota((TILE, OWN * (ONE + TWO)), 0) + step * TILE == goal_s[0:1, :]
+            rows_s[src * ONE : (src + 1) * ONE, :] = (one_ref[src] * factor).astype(BF)
+
+    match = iota((TILE, OWN * ONE), 0) + step * TILE == goal_s[0:1, :]
     put = jnp.where(match, 1.0, 0.0).astype(BF)
-    put = jnp.concatenate([put, put[:, OWN * ONE :]], axis=1)
-    total = excess_ref[...].astype(F32) + lag(nn_dot(put, rows_s[...]))
+    arrived = sum_s[pl.ds(pl.multiple_of(step * TILE, TILE), TILE), :]
+    total = excess_ref[...].astype(F32) + lag(nn_dot(put, rows_s[...]) + arrived)
     high = total.astype(BF)
     low = (total - high.astype(F32)).astype(BF)
     half = HRS // 2
@@ -490,14 +561,14 @@
 ):
     lists = (send_rows, send_owner, send_down)
     fields = (depth_start, conveyance, cell_rain, flow_dir)
+    anywhere = pl.BlockSpec(memory_space=pl.ANY)
     whole = lambda shape: pl.BlockSpec(shape, lambda i: (0,) * len(shape))
-    table, rank, columns, last, initial = pl.pallas_call(
+    table, rank, last, initial = pl.pallas_call(
         front_kernel,
         grid=(1,),
         out_shape=[
             jax.ShapeDtypeStruct((OWN, TABLE, LIST), F32),
             jax.ShapeDtypeStruct((8, ENT), I32),
-            jax.ShapeDtypeStruct((LIST, LIST), I32),
             jax.ShapeDtypeStruct((4, 4, COLS), F32),
             jax.ShapeDtypeStruct((4, 4, COLS), F32),
         ],
@@ -507,7 +578,6 @@
         out_specs=[
             whole((OWN, TABLE, LIST)),
             whole((8, ENT)),
-            whole((LIST, LIST)),
             whole((4, 4, COLS)),
             whole((4, 4, COLS)),
         ],
@@ -521,32 +591,46 @@
         gather_kernel,
         out_shape=jax.ShapeDtypeStruct((OWN, ONE, HRS), F32),
         grid=(1,),
-        in_specs=[whole(x.shape) for x in (columns, rain_hours)],
+        in_specs=[whole(x.shape) for x in (*lists, rain_hours)],
         out_specs=whole((OWN, ONE, HRS)),
+        scratch_shapes=[pltpu.VMEM((LIST, LIST), I32)],
+        compiler_params=ROOM,
         name="gather_rain",
-    )(columns, rain_hours)
+    )(*lists, rain_hours)
     arrived = exchange(outgoing)
     west_strip, east_strip = pl.pallas_call(
         strip_kernel,
         out_shape=[jax.ShapeDtypeStruct((EXT_R, 128), F32)] * 2,
         grid=(1,),
-        in_specs=[whole(x.shape) for x in (*fields, north, south)],
+        in_specs=[whole(x.shape) for x in fields] + [anywhere] * 2,
         out_specs=[whole((EXT_R, 128))] * 2,
+        scratch_shapes=[pltpu.VMEM((4, 4, COLS), F32)] * 2 + [pltpu.SemaphoreType.DMA((2,))],
+        compiler_params=ROOM,
         name="strips",
     )(*fields, north, south)
     up, down = neighbours("narrow")
     west = lax.ppermute(east_strip, "narrow", up)
     east = lax.ppermute(west_strip, "narrow", down)
-    columns, left, meta = pl.pallas_call(
+    columns, hops, goals, left, meta = pl.pallas_call(
         plan_kernel,
         out_shape=[
             jax.ShapeDtypeStruct((LIST, LIST), I32),
+            jax.ShapeDtypeStruct((LIST, LIST), I32),
+            jax.ShapeDtypeStruct((OWN, LIST), F32),
             jax.ShapeDtypeStruct((16, ENT), I32),
             jax.ShapeDtypeStruct((OWN, HRS), F32),
         ],
         grid=(1,),
-        in_specs=[whole(x.shape) for x in (*lists, rank, full)],
-        out_specs=[whole((LIST, LIST)), whole((16, ENT)), whole((OWN, HRS))],
+        in_specs=[whole(x.shape) for x in (*lists, rank)] + [pl.BlockSpec(memory_space=pl.ANY)],
+        out_specs=[
+            whole((LIST, LIST)),
+            whole((LIST, LIST)),
+            whole((OWN, LIST)),
+            whole((16, ENT)),
+            whole((OWN, HRS)),
+        ],
+        scratch_shapes=[pltpu.VMEM((OWN, TABLE, LIST), F32)],
+        compiler_params=ROOM,
         name="plan",
     )(*lists, rank, full)
     kernel = unit_hydro.astype(BF)
@@ -554,7 +638,7 @@
     repeated = jnp.tile(pattern, HRS)[: HRS * (2 * HRS - 1)]
     toeplitz = repeated.reshape(HRS, 2 * HRS - 1)[:, :HRS]
     flow_inputs = (*fields, north, south, west, east, nitrogen, rain_hours)
-    flow_inputs += (*lists, rank, columns, meta)
+    flow_inputs += (*lists, rank, columns, hops, meta)
     water, nitrogen_left, excess, outgoing = pl.pallas_call(
         main_kernel,
         out_shape=[
@@ -564,7 +648,7 @@
             jax.ShapeDtypeStruct((OWN, TWO, HRS), F32),
         ],
         grid=(1,),
-        in_specs=[whole(x.shape) for x in flow_inputs],
+        in_specs=[anywhere if 4 <= k < 8 else whole(x.shape) for k, x in enumerate(flow_inputs)],
         out_specs=[
             whole((ROWS, COLS)),
             whole((ROWS, COLS)),
@@ -573,7 +657,10 @@
         ],
         scratch_shapes=[pltpu.VMEM((EXT_R, EXT_C), F32)] * 5
         + [pltpu.VMEM((EXT_R + 16, EXT_C), F32)] * 2
-        + [pltpu.VMEM((ROWS, COLS), F32)],
+        + [pltpu.VMEM((ROWS, COLS), F32)]
+        + [pltpu.VMEM((4, 4, COLS), F32)] * 2
+        + [pltpu.VMEM((EXT_R, 128), F32)] * 2
+        + [pltpu.SemaphoreType.DMA((4,))],
         name="flow_and_send",
     )(*flow_inputs)
     incoming = exchange(outgoing)
@@ -588,7 +675,7 @@
         in_specs=[
             whole((OWN, ONE, HRS)),
             whole((OWN, TWO, HRS)),
-            whole((OWN, TABLE, LIST)),
+            whole((OWN, LIST)),
             pl.BlockSpec((TILE, HRS), tile),
             whole((HRS, HRS)),
         ],
@@ -597,11 +684,15 @@
             pl.BlockSpec((1, 1), lambda i: (0, 0), memory_space=pltpu.SMEM),
         ],
         scratch_shapes=[
-            pltpu.VMEM((OWN * (ONE + 2 * TWO), HRS), BF),
-            pltpu.VMEM((8, OWN * (ONE + TWO)), I32),
-        ],
+            pltpu.VMEM((OWN * ONE, HRS), BF),
+            pltpu.VMEM((OWN, LIST), I32),
+            pltpu.VMEM((8, OWN * ONE), I32),
+            pltpu.VMEM((SUBS + 8, HRS), F32),
+            pltpu.SMEM((OWN, LIST), I32),
+        ],
+        compiler_params=pltpu.CompilerParams(vmem_limit_bytes=50 << 20),
         name="route_and_convolve",
-    )(arrived, incoming, full, excess, toeplitz)
+    )(arrived, incoming, goals, excess, toeplitz)
 
     def more(state):
         return state[0] * EXTRA < most_left[0, 0]

time: 122 us -> 117 us (0.959)
  Pallas kernels: 34.9 us -> 28.9 us
  waiting for transfers between devices: 43 us -> 41.1 us
  local copies, waits for them, and re-layouts: 9.47 us -> 11.1 us
    pallas_call x1, Pallas kernels: 5.33 us -> 2.81 us  [routed_local(): pl.pallas_call(gather_kernel, out_shape=jax.ShapeDtypeStruct((OWN, ONE, H...]
    pallas_call x1, Pallas kernels: 12.4 us -> 10.3 us  [routed_local(): pl.pallas_call(final_kernel, out_shape=[jax.ShapeDtypeStruct((SUBS, HRS),...]
    all_to_all x3, waiting for transfers between devices: 38.3 us -> 36.4 us  [exchange(): lax.all_to_all(array, 'wide', split_axis=0, concat_axis=0, tiled=True)]
    pallas_call x1, Pallas kernels: 9.41 us -> 11.2 us  [routed_local(): pl.pallas_call(main_kernel, out_shape=[jax.ShapeDtypeStruct((ROWS, COLS),...]
    pallas_call x1, Pallas kernels: 2.03 us -> 0.32 us  [routed_local(): pl.pallas_call(strip_kernel, out_shape=[jax.ShapeDtypeStruct((EXT_R, 128)...]
    pallas_call x1, Pallas kernels: 3.68 us -> 2.31 us  [routed_local(): pl.pallas_call(plan_kernel, out_shape=[jax.ShapeDtypeStruct((LIST, LIST),...]
    unnamed x24 -> x44, local copies, waits for them, and re-layouts: 5.71 us -> 5.38 us
  transfers between devices with their start and end apart: 7 -> 7, of which waited for: 4 -> 4; matrix products, arithmetic and copies ran while one was open for 7% -> 10% of each run, Pallas kernels for 9% -> 5%
where the time goes in v3:
time: 117 us; the launch traced here: 116 us
  waiting for transfers between devices  41.1 us (35%)
  Pallas kernels  28.9 us (25%)
  starting transfers between devices  28.6 us (24%)
  local copies, waits for them, and re-layouts  11.1 us (9%)
  matrix products  4.21 us (4%)
    all_to_all x3, waiting for transfers between devices, exchange(): lax.all_to_all(array, 'wide', split_axis=0, concat_axis=0, tiled=True)  36.4 us
    all_to_all x3, starting transfers between devices, exchange(): lax.all_to_all(array, 'wide', split_axis=0, concat_axis=0, tiled=True)  20.9 us
    pallas_call x1, Pallas kernels, routed_local(): pl.pallas_call(main_kernel, out_shape=[jax.ShapeDtypeStruct((ROWS, COLS),...  11.2 us
    pallas_call x1, Pallas kernels, routed_local(): pl.pallas_call(final_kernel, out_shape=[jax.ShapeDtypeStruct((SUBS, HRS),...  10.3 us
    unnamed x44, local copies, waits for them, and re-layouts  5.38 us
    dot_general x1, matrix products, exact_dot(): return jnp.dot(left, right, precision=EXACT, preferred_element_type=F32)  4.21 us
    ppermute x1, waiting for transfers between devices, routed_local(): south = lax.ppermute(initial, 'wide', down)  4.12 us
    reshape x1, local copies, waits for them, and re-layouts, routed_local(): toeplitz = repeated.reshape(HRS, 2 * HRS - 1)[:, :HRS]  3.86 us
  transfers between devices with their start and end apart: 7, of which 4 were waited for; matrix products, arithmetic and copies ran while one was open for 10% of the time, Pallas kernels for 5%

profile of v3, /device:TPU:0, one launch (start us, length us, event | category | flops | bytes accessed | tf_op | source)
XLA Modules:
  0.0 115.8 jit_solution(13568978352399477552)
XLA Ops:
  0.6 0.0 copy-start.15
  0.6 0.0 copy-start.13
  0.7 0.0 copy-start.4
  0.7 2.0 %front.1 = (f32[16,24,128]{2,1,0:T(8,128)}, s32[8,640]{1,0:T(8,128)}, f32[4,4,512]{2,1,0:T(4,128)}, f32[4,4,512]{2,1,0:T(4,128)}) custom-call(s32[1,5,1,128]{3,2,1,0:T(1,128)} %rows_ref.7, s32[1,5,1,128]{3,2,1,0:T(1,128)} %owner_ref.7, s32[1,5,1,128]{3,2,1,0:T(1,128)} %down_ref.7, f32[128,512]{1,0:T(8,128)} %d_ref.3, f32[128,512]{1,0:T(8,128)} %c_ref.3, ...), custom_call_target="tpu_custom_call" | custom-call | tf_op jit(solution)/shard_map/front/pallas_call | solution.py:566
  2.7 8.0 %all-to-all-start.2 = ((f32[16,24,128]{2,1,0:T(8,128)}), f32[16,24,128]{2,1,0:T(8,128)S(1)}, u32[]{:S(2)}, u32[]{:S(2)}) async-start(f32[16,24,128]{2,1,0:T(8,128)} %get-tuple-element.234), calls=%async_computation.2 | async-start | bytes 393216 | tf_op jit(solution)/shard_map/all_to_all | solution.py:543
  10.7 3.8 %collective-permute-start = (f32[4,4,512]{2,1,0:T(4,128)}, f32[4,4,512]{2,1,0:T(4,128)S(1)}, u32[]{:S(2)}, u32[]{:S(2)}) collective-permute-start(f32[4,4,512]{2,1,0:T(4,128)} %get-tuple-element.229), channel_id=1, source_target_pairs={{0,8},{8,16},{16,24},{24,32},{32,40},{40,48},{48,56},{56,64},{64,7... | collective-permute-start | bytes 98312 | tf_op jit(solution)/shard_map/ppermute | solution.py:588
  14.6 1.3 %collective-permute-start.1 = (f32[4,4,512]{2,1,0:T(4,128)}, f32[4,4,512]{2,1,0:T(4,128)S(1)}, u32[]{:S(2)}, u32[]{:S(2)}) collective-permute-start(f32[4,4,512]{2,1,0:T(4,128)} %get-tuple-element.230), channel_id=1, source_target_pairs={{8,0},{16,8},{24,16},{32,24},{40,32},{48,40},{56,48},{64,56},{72,6... | collective-permute-start | bytes 98312 | tf_op jit(solution)/shard_map/ppermute | solution.py:589
  15.9 0.6 collective-permute-done.north_any
  16.4 4.1 %collective-permute-done.1.south_any = f32[4,4,512]{2,1,0:T(4,128)S(1)} collective-permute-done((f32[4,4,512]{2,1,0:T(4,128)}, f32[4,4,512]{2,1,0:T(4,128)S(1)}, u32[]{:S(2)}, u32[]{:S(2)}) %collective-permute-start.1) | collective-permute-done | bytes 32800 | tf_op jit(solution)/shard_map/ppermute | solution.py:589
  20.6 0.3 strips.1
  20.9 1.3 %collective-permute-start.2 = (f32[144,128]{1,0:T(8,128)S(1)}, f32[144,128]{1,0:T(8,128)S(1)}, u32[]{:S(2)}, u32[]{:S(2)}) collective-permute-start(f32[144,128]{1,0:T(8,128)S(1)} %get-tuple-element.231), channel_id=1, source_target_pairs={{0,1},{1,2},{2,3},{3,4},{4,5},{5,6},{6,7},{8,9},{9,10},{10,11},{11... | collective-permute-start | bytes 221192 | tf_op jit(solution)/shard_map/ppermute | solution.py:612
  22.2 1.3 %collective-permute-start.3 = (f32[144,128]{1,0:T(8,128)S(1)}, f32[144,128]{1,0:T(8,128)S(1)}, u32[]{:S(2)}, u32[]{:S(2)}) collective-permute-start(f32[144,128]{1,0:T(8,128)S(1)} %get-tuple-element.232), channel_id=1, source_target_pairs={{1,0},{2,1},{3,2},{4,3},{5,4},{6,5},{7,6},{9,8},{10,9},{11,10},{12... | collective-permute-start | bytes 221192 | tf_op jit(solution)/shard_map/ppermute | solution.py:613
  23.6 2.3 %plan.1 = (s32[128,128]{1,0:T(8,128)S(1)}, s32[128,128]{1,0:T(8,128)S(1)}, f32[16,128]{1,0:T(8,128)S(1)}, s32[16,640]{1,0:T(8,128)S(1)}, f32[16,512]{1,0:T(8,128)S(1)}) custom-call(s32[1,5,1,128]{3,2,1,0:T(1,128)S(1)} %copy-done.11, s32[1,5,1,128]{3,2,1,0:T(1,128)S(1)} %copy-done.13, s32[1,5,1,128]{3,2,1,0:T(1,128)S(1)} %copy-done.15, ...), custom_call_target="tpu_custom_call" | custom-call | tf_op jit(solution)/shard_map/plan/pallas_call | solution.py:614
  25.9 0.6 copy-done.9
  26.5 0.6 copy-done.10
  27.2 0.6 copy-done.17
  27.8 0.6 copy-done.20
  28.4 0.0 copy-done.21
  28.4 11.2 %flow_and_send.1 = (f32[128,512]{1,0:T(8,128)}, f32[128,512]{1,0:T(8,128)}, bf16[2048,512]{1,0:T(8,128)(2,1)}, f32[16,32,512]{2,1,0:T(8,128)}) custom-call(f32[128,512]{1,0:T(8,128)} %d_ref.3, f32[128,512]{1,0:T(8,128)} %c_ref.3, f32[128,512]{1,0:T(8,128)} %r_ref.3, s32[128,512]{1,0:T(8,128)} %f_ref.3, f32[4,4,512]{2,1,0:T(4,128)} %copy-done.6, ...), custom_call_target="tpu_custom_call" | custom-call | tf_op jit(solution)/shard_map/flow_and_send/pallas_call | solution.py:642
  39.7 8.4 %all-to-all-start.4 = ((f32[16,32,512]{2,1,0:T(8,128)}), f32[16,32,512]{2,1,0:T(8,128)S(1)}, u32[]{:S(2)}, u32[]{:S(2)}) async-start(f32[16,32,512]{2,1,0:T(8,128)} %get-tuple-element.240), calls=%async_computation.4 | async-start | bytes 2097152 | tf_op jit(solution)/shard_map/all_to_all | solution.py:543
  48.1 2.8 %gather_rain.1 = f32[16,64,512]{2,1,0:T(8,128)S(1)} custom-call(s32[1,5,1,128]{3,2,1,0:T(1,128)S(1)} %copy-done.12, s32[1,5,1,128]{3,2,1,0:T(1,128)S(1)} %copy-done.14, s32[1,5,1,128]{3,2,1,0:T(1,128)S(1)} %copy-done.16, bf16[1,2048,512]{2,1,0:T(8,128)(2,1)S(1)} %copy-done), custom_call_target="tpu_custom_call" | custom-call | tf_op jit(solution)/shard_map/gather_rain/pallas_call | solution.py:590
  51.0 1.3 %copy-done.1 = f32[16,64,512]{2,1,0:T(8,128)} copy-done((f32[16,64,512]{2,1,0:T(8,128)}, f32[16,64,512]{2,1,0:T(8,128)S(1)}, u32[]{:S(2)}) %copy-start.1) | copy-done | bytes 2097176
  52.3 12.7 %all-to-all-done.4.two_ref = f32[16,32,512]{2,1,0:T(8,128)S(1)} async-done(((f32[16,32,512]{2,1,0:T(8,128)}), f32[16,32,512]{2,1,0:T(8,128)S(1)}, u32[]{:S(2)}, u32[]{:S(2)}) %all-to-all-start.4) | async-done | bytes 1048608 | tf_op jit(solution)/shard_map/all_to_all | solution.py:543
  65.0 4.5 %all-to-all-start.3 = ((f32[16,64,512]{2,1,0:T(8,128)}), f32[16,64,512]{2,1,0:T(8,128)S(1)}, u32[]{:S(2)}, u32[]{:S(2)}) async-start(f32[16,64,512]{2,1,0:T(8,128)} %copy-done.1), calls=%async_computation.3 | async-start | bytes 4194304 | tf_op jit(solution)/shard_map/all_to_all | solution.py:543
  69.6 0.2 broadcast_bitcast_fusion
  69.9 1.3 %copy.13 = bf16[64,8,8,128]{3,1,2,0:T(8,128)(2,1)} copy(bf16[64,8,8,128]{3,2,1,0:T(8,128)(2,1)S(1)} %broadcast_bitcast_fusion) | data formatting | bytes 2097152
  71.1 3.9 %reshape.173 = bf16[512,1023]{1,0:T(8,128)(2,1)} reshape(bf16[523776]{0:T(1024)(128)(2,1)} %bitcast.47) | data formatting | bytes 2095104 | tf_op jit(solution)/shard_map/reshape | solution.py:639
  75.0 1.9 %slice.174.kernel_ref = bf16[512,512]{1,0:T(8,128)(2,1)} slice(bf16[512,1023]{1,0:T(8,128)(2,1)} %reshape.173), slice={[0:512], [0:512]} | slice | bytes 1048576 | tf_op jit(solution)/shard_map/slice | solution.py:639
  76.9 4.2 %fusion.44 = f32[640,512]{1,0:T(8,128)} fusion(bf16[2048,512]{1,0:T(8,128)(2,1)} %get-tuple-element.242.excess_ref, s32[640]{0:T(1024)S(1)} %bitcast_select_fusion), kind=kOutput, calls=%fused_computation.83 | convolution fusion | flops 1343488000 | bytes 3410432 | tf_op jit(solution)/shard_map/while/body/dot_general | solution.py:547
  81.1 23.7 %all-to-all-done.3.one_ref = f32[16,64,512]{2,1,0:T(8,128)S(1)} async-done(((f32[16,64,512]{2,1,0:T(8,128)}), f32[16,64,512]{2,1,0:T(8,128)S(1)}, u32[]{:S(2)}, u32[]{:S(2)}) %all-to-all-start.3) | async-done | bytes 2097184 | tf_op jit(solution)/shard_map/all_to_all | solution.py:543
  104.8 10.3 %route_and_convolve.1 = (f32[2048,512]{1,0:T(8,128)}, s32[1,1]{1,0:T(1,128)}) custom-call(f32[16,64,512]{2,1,0:T(8,128)S(1)} %all-to-all-done.3.one_ref, f32[16,32,512]{2,1,0:T(8,128)S(1)} %all-to-all-done.4.two_ref, f32[16,128]{1,0:T(8,128)S(1)} %get-tuple-element.241.goal_ref, bf16[2048,512]{1,0:T(8,128)(2,1)} %get-tuple-element.242.excess_ref, ...), custom_call_target="tpu_custom_call" | custom-call | tf_op jit(solution)/shard_map/route_and_convolve/pallas_call | solution.py:668
  115.0 0.6 while.14
  (41 shorter events, 0.2 us)
Async XLA Ops:
  0.6 22.9 %copy-start.15 = (s32[1,5,1,128]{3,2,1,0:T(1,128)S(1)}, s32[1,5,1,128]{3,2,1,0:T(1,128)}, u32[]{:S(2)}) copy-start(s32[1,5,1,128]{3,2,1,0:T(1,128)} %down_ref.7) | copy-start | bytes 7684
  0.6 22.9 %copy-start.13 = (s32[1,5,1,128]{3,2,1,0:T(1,128)S(1)}, s32[1,5,1,128]{3,2,1,0:T(1,128)}, u32[]{:S(2)}) copy-start(s32[1,5,1,128]{3,2,1,0:T(1,128)} %owner_ref.7) | copy-start | bytes 7684
  0.7 22.9 %copy-start.11 = (s32[1,5,1,128]{3,2,1,0:T(1,128)S(1)}, s32[1,5,1,128]{3,2,1,0:T(1,128)}, u32[]{:S(2)}) copy-start(s32[1,5,1,128]{3,2,1,0:T(1,128)} %rows_ref.7) | copy-start | bytes 7684
  0.7 19.9 %copy-start.5 = (s32[128,512]{1,0:T(8,128)S(1)}, s32[128,512]{1,0:T(8,128)}, u32[]{:S(2)}) copy-start(s32[128,512]{1,0:T(8,128)} %f_ref.3) | copy-start | bytes 786436
  0.7 19.9 %copy-start.4 = (f32[128,512]{1,0:T(8,128)S(1)}, f32[128,512]{1,0:T(8,128)}, u32[]{:S(2)}) copy-start(f32[128,512]{1,0:T(8,128)} %r_ref.3) | copy-start | bytes 786436
  0.7 19.9 %copy-start.3 = (f32[128,512]{1,0:T(8,128)S(1)}, f32[128,512]{1,0:T(8,128)}, u32[]{:S(2)}) copy-start(f32[128,512]{1,0:T(8,128)} %c_ref.3) | copy-start | bytes 786436
  0.7 19.9 %copy-start.2 = (f32[128,512]{1,0:T(8,128)S(1)}, f32[128,512]{1,0:T(8,128)}, u32[]{:S(2)}) copy-start(f32[128,512]{1,0:T(8,128)} %d_ref.3) | copy-start | bytes 786436
  2.7 20.9 %copy-start.8 = (s32[8,640]{1,0:T(8,128)S(1)}, s32[8,640]{1,0:T(8,128)}, u32[]{:S(2)}) copy-start(s32[8,640]{1,0:T(8,128)} %get-tuple-element.233.rank_ref) | copy-start | bytes 61444
  2.7 20.8 %all-to-all-start.2 = ((f32[16,24,128]{2,1,0:T(8,128)}), f32[16,24,128]{2,1,0:T(8,128)S(1)}, u32[]{:S(2)}, u32[]{:S(2)}) async-start(f32[16,24,128]{2,1,0:T(8,128)} %get-tuple-element.234), calls=%async_computation.2 | async-start | bytes 393216 | tf_op jit(solution)/shard_map/all_to_all | solution.py:543
  10.7 5.7 %collective-permute-start = (f32[4,4,512]{2,1,0:T(4,128)}, f32[4,4,512]{2,1,0:T(4,128)S(1)}, u32[]{:S(2)}, u32[]{:S(2)}) collective-permute-start(f32[4,4,512]{2,1,0:T(4,128)} %get-tuple-element.229), channel_id=1, source_target_pairs={{0,8},{8,16},{16,24},{24,32},{32,40},{40,48},{48,56},{56,64},{64,7... | collective-permute-start | bytes 98312 | tf_op jit(solution)/shard_map/ppermute | solution.py:588
  14.6 6.0 %collective-permute-start.1 = (f32[4,4,512]{2,1,0:T(4,128)}, f32[4,4,512]{2,1,0:T(4,128)S(1)}, u32[]{:S(2)}, u32[]{:S(2)}) collective-permute-start(f32[4,4,512]{2,1,0:T(4,128)} %get-tuple-element.230), channel_id=1, source_target_pairs={{8,0},{16,8},{24,16},{32,24},{40,32},{48,40},{56,48},{64,56},{72,6... | collective-permute-start | bytes 98312 | tf_op jit(solution)/shard_map/ppermute | solution.py:589
  16.4 11.3 %copy-start.6 = (f32[4,4,512]{2,1,0:T(4,128)}, f32[4,4,512]{2,1,0:T(4,128)S(1)}, u32[]{:S(2)}) copy-start(f32[4,4,512]{2,1,0:T(4,128)S(1)} %collective-permute-done.north_any) | copy-start | bytes 98308
  20.6 7.2 %copy-start.7 = (f32[4,4,512]{2,1,0:T(4,128)}, f32[4,4,512]{2,1,0:T(4,128)S(1)}, u32[]{:S(2)}) copy-start(f32[4,4,512]{2,1,0:T(4,128)S(1)} %collective-permute-done.1.south_any) | copy-start | bytes 98308
  20.9 6.8 %collective-permute-start.2 = (f32[144,128]{1,0:T(8,128)S(1)}, f32[144,128]{1,0:T(8,128)S(1)}, u32[]{:S(2)}, u32[]{:S(2)}) collective-permute-start(f32[144,128]{1,0:T(8,128)S(1)} %get-tuple-element.231), channel_id=1, source_target_pairs={{0,1},{1,2},{2,3},{3,4},{4,5},{5,6},{6,7},{8,9},{9,10},{10,11},{11... | collective-permute-start | bytes 221192 | tf_op jit(solution)/shard_map/ppermute | solution.py:612
  22.2 5.5 %collective-permute-start.3 = (f32[144,128]{1,0:T(8,128)S(1)}, f32[144,128]{1,0:T(8,128)S(1)}, u32[]{:S(2)}, u32[]{:S(2)}) collective-permute-start(f32[144,128]{1,0:T(8,128)S(1)} %get-tuple-element.232), channel_id=1, source_target_pairs={{1,0},{2,1},{3,2},{4,3},{5,4},{6,5},{7,6},{9,8},{10,9},{11,10},{12... | collective-permute-start | bytes 221192 | tf_op jit(solution)/shard_map/ppermute | solution.py:613
  25.9 0.6 copy-start.9
  26.5 0.6 copy-start.10
  27.2 0.6 copy-start.17
  27.8 0.6 copy-start.20
  27.8 0.6 copy-start.21
  28.4 19.7 %copy-start.12 = (s32[1,5,1,128]{3,2,1,0:T(1,128)S(1)}, s32[1,5,1,128]{3,2,1,0:T(1,128)}, u32[]{:S(2)}) copy-start(s32[1,5,1,128]{3,2,1,0:T(1,128)} %rows_ref.7) | copy-start | bytes 7684
  28.4 19.7 %copy-start.14 = (s32[1,5,1,128]{3,2,1,0:T(1,128)S(1)}, s32[1,5,1,128]{3,2,1,0:T(1,128)}, u32[]{:S(2)}) copy-start(s32[1,5,1,128]{3,2,1,0:T(1,128)} %owner_ref.7) | copy-start | bytes 7684
  28.4 19.7 %copy-start.16 = (s32[1,5,1,128]{3,2,1,0:T(1,128)S(1)}, s32[1,5,1,128]{3,2,1,0:T(1,128)}, u32[]{:S(2)}) copy-start(s32[1,5,1,128]{3,2,1,0:T(1,128)} %down_ref.7) | copy-start | bytes 7684
  39.7 8.5 %copy-start = (bf16[1,2048,512]{2,1,0:T(8,128)(2,1)S(1)}, bf16[1,2048,512]{2,1,0:T(8,128)(2,1)}, u32[]{:S(2)}) copy-start(bf16[1,2048,512]{2,1,0:T(8,128)(2,1)} %hours_ref.3) | copy-start | bytes 6291460
  39.7 25.4 %all-to-all-start.4 = ((f32[16,32,512]{2,1,0:T(8,128)}), f32[16,32,512]{2,1,0:T(8,128)S(1)}, u32[]{:S(2)}, u32[]{:S(2)}) async-start(f32[16,32,512]{2,1,0:T(8,128)} %get-tuple-element.240), calls=%async_computation.4 | async-start | bytes 2097152 | tf_op jit(solution)/shard_map/all_to_all | solution.py:543
  51.0 1.3 %copy-start.1 = (f32[16,64,512]{2,1,0:T(8,128)}, f32[16,64,512]{2,1,0:T(8,128)S(1)}, u32[]{:S(2)}) copy-start(f32[16,64,512]{2,1,0:T(8,128)S(1)} %gather_rain.1) | copy-start | bytes 6291460
  52.3 17.3 %copy-start.22 = (f32[512]{0:T(512)S(1)}, f32[512]{0:T(512)}, u32[]{:S(2)}) copy-start(f32[512]{0:T(512)} %param.17) | copy-start | bytes 6148
  65.0 39.7 %all-to-all-start.3 = ((f32[16,64,512]{2,1,0:T(8,128)}), f32[16,64,512]{2,1,0:T(8,128)S(1)}, u32[]{:S(2)}, u32[]{:S(2)}) async-start(f32[16,64,512]{2,1,0:T(8,128)} %copy-done.1), calls=%async_computation.3 | async-start | bytes 4194304 | tf_op jit(solution)/shard_map/all_to_all | solution.py:543

commit v4 on v3

--- a/solution.py
+++ b/solution.py
@@ -486,6 +486,7 @@
     goal_s,
     sum_s,
     target_s,
+    sem,
 ):
     step = pl.program_id(0)
 
@@ -494,18 +495,9 @@
         groups = [two_ref[src, TWO - 8 : TWO, :][7:8] for src in range(OWN)]
         for src in range(OWN):
             line_s[src : src + 1, :] = groups[src][:, 0:128].astype(I32) - 1
-        pltpu.sync_copy(line_s, target_s)
+        targets = pltpu.make_async_copy(line_s, target_s, sem)
+        targets.start()
         sum_s[...] = jnp.zeros(sum_s.shape, F32)
-        for src in range(OWN):
-
-            def add_row(slot, carry):
-                target = target_s[src, slot]
-                target = jnp.where(target >= 0, target, SUBS)
-                row = two_ref[src, pl.ds(slot, 1), :]
-                sum_s[pl.ds(target, 1), :] = sum_s[pl.ds(target, 1), :] + row
-                return carry
-
-            lax.fori_loop(0, target_s[src, LIST - 1], add_row, 0)
         goal_s[...] = flat_line(
             [jnp.broadcast_to(goal_ref[src : src + 1, :], (8, 128)) for src in range(OWN)], ONE
         )
@@ -518,6 +510,17 @@
             factor = jnp.broadcast_to(factors[0:ONE, src : src + 1], (ONE, 128))
             factor = jnp.concatenate([factor] * (HRS // 128), axis=1)
             rows_s[src * ONE : (src + 1) * ONE, :] = (one_ref[src] * factor).astype(BF)
+        targets.wait()
+        for src in range(OWN):
+
+            def add_row(slot, carry):
+                target = target_s[src, slot]
+                target = jnp.where(target >= 0, target, SUBS)
+                row = two_ref[src, pl.ds(slot, 1), :]
+                sum_s[pl.ds(target, 1), :] = sum_s[pl.ds(target, 1), :] + row
+                return carry
+
+            lax.fori_loop(0, target_s[src, LIST - 1], add_row, 0)
 
     match = iota((TILE, OWN * ONE), 0) + step * TILE == goal_s[0:1, :]
     put = jnp.where(match, 1.0, 0.0).astype(BF)
@@ -689,6 +692,7 @@
             pltpu.VMEM((8, OWN * ONE), I32),
             pltpu.VMEM((SUBS + 8, HRS), F32),
             pltpu.SMEM((OWN, LIST), I32),
+            pltpu.SemaphoreType.DMA,
         ],
         compiler_params=pltpu.CompilerParams(vmem_limit_bytes=50 << 20),
         name="route_and_convolve",

time: 117 us -> 117 us (level)
  no operation moved by 1% of the time
where the time goes in v4:
time: 117 us; the launch traced here: 116 us
  waiting for transfers between devices  41.1 us (35%)
  Pallas kernels  28.7 us (25%)
  starting transfers between devices  28.6 us (24%)
  local copies, waits for them, and re-layouts  11.1 us (9%)
  matrix products  4.21 us (4%)
    all_to_all x3, waiting for transfers between devices, exchange(): lax.all_to_all(array, 'wide', split_axis=0, concat_axis=0, tiled=True)  36.4 us
    all_to_all x3, starting transfers between devices, exchange(): lax.all_to_all(array, 'wide', split_axis=0, concat_axis=0, tiled=True)  20.9 us
    pallas_call x1, Pallas kernels, routed_local(): pl.pallas_call(main_kernel, out_shape=[jax.ShapeDtypeStruct((ROWS, COLS),...  11.2 us
    pallas_call x1, Pallas kernels, routed_local(): pl.pallas_call(final_kernel, out_shape=[jax.ShapeDtypeStruct((SUBS, HRS),...  10.1 us
    unnamed x44, local copies, waits for them, and re-layouts  5.38 us
    dot_general x1, matrix products, exact_dot(): return jnp.dot(left, right, precision=EXACT, preferred_element_type=F32)  4.21 us
    ppermute x1, waiting for transfers between devices, routed_local(): south = lax.ppermute(initial, 'wide', down)  4.12 us
    reshape x1, local copies, waits for them, and re-layouts, routed_local(): toeplitz = repeated.reshape(HRS, 2 * HRS - 1)[:, :HRS]  3.86 us
  transfers between devices with their start and end apart: 7, of which 4 were waited for; matrix products, arithmetic and copies ran while one was open for 10% of the time, Pallas kernels for 5%

profile of v4, /device:TPU:0, one launch (start us, length us, event | category | flops | bytes accessed | tf_op | source)
XLA Modules:
  0.0 115.7 jit_solution(5340854565364639188)
XLA Ops:
  0.6 0.0 copy-start.15
  0.6 0.0 copy-start.13
  0.7 0.0 copy-start.4
  0.7 2.0 %front.1 = (f32[16,24,128]{2,1,0:T(8,128)}, s32[8,640]{1,0:T(8,128)}, f32[4,4,512]{2,1,0:T(4,128)}, f32[4,4,512]{2,1,0:T(4,128)}) custom-call(s32[1,5,1,128]{3,2,1,0:T(1,128)} %rows_ref.7, s32[1,5,1,128]{3,2,1,0:T(1,128)} %owner_ref.7, s32[1,5,1,128]{3,2,1,0:T(1,128)} %down_ref.7, f32[128,512]{1,0:T(8,128)} %d_ref.3, f32[128,512]{1,0:T(8,128)} %c_ref.3, ...), custom_call_target="tpu_custom_call" | custom-call | tf_op jit(solution)/shard_map/front/pallas_call | solution.py:569
  2.7 8.0 %all-to-all-start.2 = ((f32[16,24,128]{2,1,0:T(8,128)}), f32[16,24,128]{2,1,0:T(8,128)S(1)}, u32[]{:S(2)}, u32[]{:S(2)}) async-start(f32[16,24,128]{2,1,0:T(8,128)} %get-tuple-element.234), calls=%async_computation.2 | async-start | bytes 393216 | tf_op jit(solution)/shard_map/all_to_all | solution.py:546
  10.7 3.8 %collective-permute-start = (f32[4,4,512]{2,1,0:T(4,128)}, f32[4,4,512]{2,1,0:T(4,128)S(1)}, u32[]{:S(2)}, u32[]{:S(2)}) collective-permute-start(f32[4,4,512]{2,1,0:T(4,128)} %get-tuple-element.229), channel_id=1, source_target_pairs={{0,8},{8,16},{16,24},{24,32},{32,40},{40,48},{48,56},{56,64},{64,7... | collective-permute-start | bytes 98312 | tf_op jit(solution)/shard_map/ppermute | solution.py:591
  14.6 1.3 %collective-permute-start.1 = (f32[4,4,512]{2,1,0:T(4,128)}, f32[4,4,512]{2,1,0:T(4,128)S(1)}, u32[]{:S(2)}, u32[]{:S(2)}) collective-permute-start(f32[4,4,512]{2,1,0:T(4,128)} %get-tuple-element.230), channel_id=1, source_target_pairs={{8,0},{16,8},{24,16},{32,24},{40,32},{48,40},{56,48},{64,56},{72,6... | collective-permute-start | bytes 98312 | tf_op jit(solution)/shard_map/ppermute | solution.py:592
  15.9 0.6 collective-permute-done.north_any
  16.4 4.1 %collective-permute-done.1.south_any = f32[4,4,512]{2,1,0:T(4,128)S(1)} collective-permute-done((f32[4,4,512]{2,1,0:T(4,128)}, f32[4,4,512]{2,1,0:T(4,128)S(1)}, u32[]{:S(2)}, u32[]{:S(2)}) %collective-permute-start.1) | collective-permute-done | bytes 32800 | tf_op jit(solution)/shard_map/ppermute | solution.py:592
  20.6 0.3 strips.1
  20.9 1.3 %collective-permute-start.2 = (f32[144,128]{1,0:T(8,128)S(1)}, f32[144,128]{1,0:T(8,128)S(1)}, u32[]{:S(2)}, u32[]{:S(2)}) collective-permute-start(f32[144,128]{1,0:T(8,128)S(1)} %get-tuple-element.231), channel_id=1, source_target_pairs={{0,1},{1,2},{2,3},{3,4},{4,5},{5,6},{6,7},{8,9},{9,10},{10,11},{11... | collective-permute-start | bytes 221192 | tf_op jit(solution)/shard_map/ppermute | solution.py:615
  22.2 1.3 %collective-permute-start.3 = (f32[144,128]{1,0:T(8,128)S(1)}, f32[144,128]{1,0:T(8,128)S(1)}, u32[]{:S(2)}, u32[]{:S(2)}) collective-permute-start(f32[144,128]{1,0:T(8,128)S(1)} %get-tuple-element.232), channel_id=1, source_target_pairs={{1,0},{2,1},{3,2},{4,3},{5,4},{6,5},{7,6},{9,8},{10,9},{11,10},{12... | collective-permute-start | bytes 221192 | tf_op jit(solution)/shard_map/ppermute | solution.py:616
  23.6 2.3 %plan.1 = (s32[128,128]{1,0:T(8,128)S(1)}, s32[128,128]{1,0:T(8,128)S(1)}, f32[16,128]{1,0:T(8,128)S(1)}, s32[16,640]{1,0:T(8,128)S(1)}, f32[16,512]{1,0:T(8,128)S(1)}) custom-call(s32[1,5,1,128]{3,2,1,0:T(1,128)S(1)} %copy-done.11, s32[1,5,1,128]{3,2,1,0:T(1,128)S(1)} %copy-done.13, s32[1,5,1,128]{3,2,1,0:T(1,128)S(1)} %copy-done.15, ...), custom_call_target="tpu_custom_call" | custom-call | tf_op jit(solution)/shard_map/plan/pallas_call | solution.py:617
  25.9 0.6 copy-done.9
  26.5 0.6 copy-done.10
  27.2 0.6 copy-done.17
  27.8 0.6 copy-done.20
  28.4 0.0 copy-done.21
  28.4 11.2 %flow_and_send.1 = (f32[128,512]{1,0:T(8,128)}, f32[128,512]{1,0:T(8,128)}, bf16[2048,512]{1,0:T(8,128)(2,1)}, f32[16,32,512]{2,1,0:T(8,128)}) custom-call(f32[128,512]{1,0:T(8,128)} %d_ref.3, f32[128,512]{1,0:T(8,128)} %c_ref.3, f32[128,512]{1,0:T(8,128)} %r_ref.3, s32[128,512]{1,0:T(8,128)} %f_ref.3, f32[4,4,512]{2,1,0:T(4,128)} %copy-done.6, ...), custom_call_target="tpu_custom_call" | custom-call | tf_op jit(solution)/shard_map/flow_and_send/pallas_call | solution.py:645
  39.7 8.4 %all-to-all-start.4 = ((f32[16,32,512]{2,1,0:T(8,128)}), f32[16,32,512]{2,1,0:T(8,128)S(1)}, u32[]{:S(2)}, u32[]{:S(2)}) async-start(f32[16,32,512]{2,1,0:T(8,128)} %get-tuple-element.240), calls=%async_computation.4 | async-start | bytes 2097152 | tf_op jit(solution)/shard_map/all_to_all | solution.py:546
  48.1 2.8 %gather_rain.1 = f32[16,64,512]{2,1,0:T(8,128)S(1)} custom-call(s32[1,5,1,128]{3,2,1,0:T(1,128)S(1)} %copy-done.12, s32[1,5,1,128]{3,2,1,0:T(1,128)S(1)} %copy-done.14, s32[1,5,1,128]{3,2,1,0:T(1,128)S(1)} %copy-done.16, bf16[1,2048,512]{2,1,0:T(8,128)(2,1)S(1)} %copy-done), custom_call_target="tpu_custom_call" | custom-call | tf_op jit(solution)/shard_map/gather_rain/pallas_call | solution.py:593
  51.0 1.3 %copy-done.1 = f32[16,64,512]{2,1,0:T(8,128)} copy-done((f32[16,64,512]{2,1,0:T(8,128)}, f32[16,64,512]{2,1,0:T(8,128)S(1)}, u32[]{:S(2)}) %copy-start.1) | copy-done | bytes 2097176
  52.3 12.7 %all-to-all-done.4.two_ref = f32[16,32,512]{2,1,0:T(8,128)S(1)} async-done(((f32[16,32,512]{2,1,0:T(8,128)}), f32[16,32,512]{2,1,0:T(8,128)S(1)}, u32[]{:S(2)}, u32[]{:S(2)}) %all-to-all-start.4) | async-done | bytes 1048608 | tf_op jit(solution)/shard_map/all_to_all | solution.py:546
  65.0 4.5 %all-to-all-start.3 = ((f32[16,64,512]{2,1,0:T(8,128)}), f32[16,64,512]{2,1,0:T(8,128)S(1)}, u32[]{:S(2)}, u32[]{:S(2)}) async-start(f32[16,64,512]{2,1,0:T(8,128)} %copy-done.1), calls=%async_computation.3 | async-start | bytes 4194304 | tf_op jit(solution)/shard_map/all_to_all | solution.py:546
  69.6 0.2 broadcast_bitcast_fusion
  69.9 1.3 %copy.13 = bf16[64,8,8,128]{3,1,2,0:T(8,128)(2,1)} copy(bf16[64,8,8,128]{3,2,1,0:T(8,128)(2,1)S(1)} %broadcast_bitcast_fusion) | data formatting | bytes 2097152
  71.1 3.9 %reshape.173 = bf16[512,1023]{1,0:T(8,128)(2,1)} reshape(bf16[523776]{0:T(1024)(128)(2,1)} %bitcast.47) | data formatting | bytes 2095104 | tf_op jit(solution)/shard_map/reshape | solution.py:642
  75.0 1.9 %slice.174.kernel_ref = bf16[512,512]{1,0:T(8,128)(2,1)} slice(bf16[512,1023]{1,0:T(8,128)(2,1)} %reshape.173), slice={[0:512], [0:512]} | slice | bytes 1048576 | tf_op jit(solution)/shard_map/slice | solution.py:642
  76.9 4.2 %fusion.44 = f32[640,512]{1,0:T(8,128)} fusion(bf16[2048,512]{1,0:T(8,128)(2,1)} %get-tuple-element.242.excess_ref, s32[640]{0:T(1024)S(1)} %bitcast_select_fusion), kind=kOutput, calls=%fused_computation.83 | convolution fusion | flops 1343488000 | bytes 3410432 | tf_op jit(solution)/shard_map/while/body/dot_general | solution.py:550
  81.1 23.7 %all-to-all-done.3.one_ref = f32[16,64,512]{2,1,0:T(8,128)S(1)} async-done(((f32[16,64,512]{2,1,0:T(8,128)}), f32[16,64,512]{2,1,0:T(8,128)S(1)}, u32[]{:S(2)}, u32[]{:S(2)}) %all-to-all-start.3) | async-done | bytes 2097184 | tf_op jit(solution)/shard_map/all_to_all | solution.py:546
  104.8 10.1 %route_and_convolve.1 = (f32[2048,512]{1,0:T(8,128)}, s32[1,1]{1,0:T(1,128)}) custom-call(f32[16,64,512]{2,1,0:T(8,128)S(1)} %all-to-all-done.3.one_ref, f32[16,32,512]{2,1,0:T(8,128)S(1)} %all-to-all-done.4.two_ref, f32[16,128]{1,0:T(8,128)S(1)} %get-tuple-element.241.goal_ref, bf16[2048,512]{1,0:T(8,128)(2,1)} %get-tuple-element.242.excess_ref, ...), custom_call_target="tpu_custom_call" | custom-call | tf_op jit(solution)/shard_map/route_and_convolve/pallas_call | solution.py:671
  114.9 0.6 while.14
  (41 shorter events, 0.2 us)
Async XLA Ops:
  0.6 22.9 %copy-start.15 = (s32[1,5,1,128]{3,2,1,0:T(1,128)S(1)}, s32[1,5,1,128]{3,2,1,0:T(1,128)}, u32[]{:S(2)}) copy-start(s32[1,5,1,128]{3,2,1,0:T(1,128)} %down_ref.7) | copy-start | bytes 7684
  0.6 22.9 %copy-start.13 = (s32[1,5,1,128]{3,2,1,0:T(1,128)S(1)}, s32[1,5,1,128]{3,2,1,0:T(1,128)}, u32[]{:S(2)}) copy-start(s32[1,5,1,128]{3,2,1,0:T(1,128)} %owner_ref.7) | copy-start | bytes 7684
  0.7 22.9 %copy-start.11 = (s32[1,5,1,128]{3,2,1,0:T(1,128)S(1)}, s32[1,5,1,128]{3,2,1,0:T(1,128)}, u32[]{:S(2)}) copy-start(s32[1,5,1,128]{3,2,1,0:T(1,128)} %rows_ref.7) | copy-start | bytes 7684
  0.7 19.9 %copy-start.5 = (s32[128,512]{1,0:T(8,128)S(1)}, s32[128,512]{1,0:T(8,128)}, u32[]{:S(2)}) copy-start(s32[128,512]{1,0:T(8,128)} %f_ref.3) | copy-start | bytes 786436
  0.7 19.9 %copy-start.4 = (f32[128,512]{1,0:T(8,128)S(1)}, f32[128,512]{1,0:T(8,128)}, u32[]{:S(2)}) copy-start(f32[128,512]{1,0:T(8,128)} %r_ref.3) | copy-start | bytes 786436
  0.7 19.9 %copy-start.3 = (f32[128,512]{1,0:T(8,128)S(1)}, f32[128,512]{1,0:T(8,128)}, u32[]{:S(2)}) copy-start(f32[128,512]{1,0:T(8,128)} %c_ref.3) | copy-start | bytes 786436
  0.7 19.9 %copy-start.2 = (f32[128,512]{1,0:T(8,128)S(1)}, f32[128,512]{1,0:T(8,128)}, u32[]{:S(2)}) copy-start(f32[128,512]{1,0:T(8,128)} %d_ref.3) | copy-start | bytes 786436
  2.7 20.9 %copy-start.8 = (s32[8,640]{1,0:T(8,128)S(1)}, s32[8,640]{1,0:T(8,128)}, u32[]{:S(2)}) copy-start(s32[8,640]{1,0:T(8,128)} %get-tuple-element.233.rank_ref) | copy-start | bytes 61444
  2.7 20.8 %all-to-all-start.2 = ((f32[16,24,128]{2,1,0:T(8,128)}), f32[16,24,128]{2,1,0:T(8,128)S(1)}, u32[]{:S(2)}, u32[]{:S(2)}) async-start(f32[16,24,128]{2,1,0:T(8,128)} %get-tuple-element.234), calls=%async_computation.2 | async-start | bytes 393216 | tf_op jit(solution)/shard_map/all_to_all | solution.py:546
  10.7 5.7 %collective-permute-start = (f32[4,4,512]{2,1,0:T(4,128)}, f32[4,4,512]{2,1,0:T(4,128)S(1)}, u32[]{:S(2)}, u32[]{:S(2)}) collective-permute-start(f32[4,4,512]{2,1,0:T(4,128)} %get-tuple-element.229), channel_id=1, source_target_pairs={{0,8},{8,16},{16,24},{24,32},{32,40},{40,48},{48,56},{56,64},{64,7... | collective-permute-start | bytes 98312 | tf_op jit(solution)/shard_map/ppermute | solution.py:591
  14.6 6.0 %collective-permute-start.1 = (f32[4,4,512]{2,1,0:T(4,128)}, f32[4,4,512]{2,1,0:T(4,128)S(1)}, u32[]{:S(2)}, u32[]{:S(2)}) collective-permute-start(f32[4,4,512]{2,1,0:T(4,128)} %get-tuple-element.230), channel_id=1, source_target_pairs={{8,0},{16,8},{24,16},{32,24},{40,32},{48,40},{56,48},{64,56},{72,6... | collective-permute-start | bytes 98312 | tf_op jit(solution)/shard_map/ppermute | solution.py:592
  16.4 11.3 %copy-start.6 = (f32[4,4,512]{2,1,0:T(4,128)}, f32[4,4,512]{2,1,0:T(4,128)S(1)}, u32[]{:S(2)}) copy-start(f32[4,4,512]{2,1,0:T(4,128)S(1)} %collective-permute-done.north_any) | copy-start | bytes 98308
  20.6 7.2 %copy-start.7 = (f32[4,4,512]{2,1,0:T(4,128)}, f32[4,4,512]{2,1,0:T(4,128)S(1)}, u32[]{:S(2)}) copy-start(f32[4,4,512]{2,1,0:T(4,128)S(1)} %collective-permute-done.1.south_any) | copy-start | bytes 98308
  20.9 6.8 %collective-permute-start.2 = (f32[144,128]{1,0:T(8,128)S(1)}, f32[144,128]{1,0:T(8,128)S(1)}, u32[]{:S(2)}, u32[]{:S(2)}) collective-permute-start(f32[144,128]{1,0:T(8,128)S(1)} %get-tuple-element.231), channel_id=1, source_target_pairs={{0,1},{1,2},{2,3},{3,4},{4,5},{5,6},{6,7},{8,9},{9,10},{10,11},{11... | collective-permute-start | bytes 221192 | tf_op jit(solution)/shard_map/ppermute | solution.py:615
  22.2 5.5 %collective-permute-start.3 = (f32[144,128]{1,0:T(8,128)S(1)}, f32[144,128]{1,0:T(8,128)S(1)}, u32[]{:S(2)}, u32[]{:S(2)}) collective-permute-start(f32[144,128]{1,0:T(8,128)S(1)} %get-tuple-element.232), channel_id=1, source_target_pairs={{1,0},{2,1},{3,2},{4,3},{5,4},{6,5},{7,6},{9,8},{10,9},{11,10},{12... | collective-permute-start | bytes 221192 | tf_op jit(solution)/shard_map/ppermute | solution.py:616
  25.9 0.6 copy-start.9
  26.5 0.6 copy-start.10
  27.2 0.6 copy-start.17
  27.8 0.6 copy-start.20
  27.8 0.6 copy-start.21
  28.4 19.7 %copy-start.12 = (s32[1,5,1,128]{3,2,1,0:T(1,128)S(1)}, s32[1,5,1,128]{3,2,1,0:T(1,128)}, u32[]{:S(2)}) copy-start(s32[1,5,1,128]{3,2,1,0:T(1,128)} %rows_ref.7) | copy-start | bytes 7684
  28.4 19.7 %copy-start.14 = (s32[1,5,1,128]{3,2,1,0:T(1,128)S(1)}, s32[1,5,1,128]{3,2,1,0:T(1,128)}, u32[]{:S(2)}) copy-start(s32[1,5,1,128]{3,2,1,0:T(1,128)} %owner_ref.7) | copy-start | bytes 7684
  28.4 19.7 %copy-start.16 = (s32[1,5,1,128]{3,2,1,0:T(1,128)S(1)}, s32[1,5,1,128]{3,2,1,0:T(1,128)}, u32[]{:S(2)}) copy-start(s32[1,5,1,128]{3,2,1,0:T(1,128)} %down_ref.7) | copy-start | bytes 7684
  39.7 8.5 %copy-start = (bf16[1,2048,512]{2,1,0:T(8,128)(2,1)S(1)}, bf16[1,2048,512]{2,1,0:T(8,128)(2,1)}, u32[]{:S(2)}) copy-start(bf16[1,2048,512]{2,1,0:T(8,128)(2,1)} %hours_ref.3) | copy-start | bytes 6291460
  39.7 25.4 %all-to-all-start.4 = ((f32[16,32,512]{2,1,0:T(8,128)}), f32[16,32,512]{2,1,0:T(8,128)S(1)}, u32[]{:S(2)}, u32[]{:S(2)}) async-start(f32[16,32,512]{2,1,0:T(8,128)} %get-tuple-element.240), calls=%async_computation.4 | async-start | bytes 2097152 | tf_op jit(solution)/shard_map/all_to_all | solution.py:546
  51.0 1.3 %copy-start.1 = (f32[16,64,512]{2,1,0:T(8,128)}, f32[16,64,512]{2,1,0:T(8,128)S(1)}, u32[]{:S(2)}) copy-start(f32[16,64,512]{2,1,0:T(8,128)S(1)} %gather_rain.1) | copy-start | bytes 6291460
  52.3 17.3 %copy-start.22 = (f32[512]{0:T(512)S(1)}, f32[512]{0:T(512)}, u32[]{:S(2)}) copy-start(f32[512]{0:T(512)} %param.17) | copy-start | bytes 6148
  65.0 39.7 %all-to-all-start.3 = ((f32[16,64,512]{2,1,0:T(8,128)}), f32[16,64,512]{2,1,0:T(8,128)S(1)}, u32[]{:S(2)}, u32[]{:S(2)}) async-start(f32[16,64,512]{2,1,0:T(8,128)} %copy-done.1), calls=%async_computation.3 | async-start | bytes 4194304 | tf_op jit(solution)/shard_map/all_to_all | solution.py:546
